TPU v7x, 32 devices: a whole 2x2x4 slice. The times are simulated.
32 devices in a mesh: tile: 8 (over y, x, core), body: 4 (over z).
Axes of the slice: x: 2, y: 2, z: 4, core: 2. Of those that a mesh axis runs over, the one named last changes fastest.
Arguments:
- fluid_position: float32 [3, 128, 32, 128], P(None, 'tile', 'body'), may hold values from 0 to 128, as said below
- fluid_pressure: float32 [128, 32, 128], P('tile', 'body'), may hold values from 0 to 1
- source: float32 [128, 32, 128], P('tile', 'body'), may hold values from -12 to 12
- stiffness: float32 [128, 32, 128], P('tile', 'body'), may hold values from 0.5 to 2
- neighbours: int32 [128, 32, 6], P('tile', 'body'), may hold values from 0 to 8, as said below
- wall_position: float32 [3, 128, 32, 128], P(None, 'tile', 'body'), may hold values from 0 to 128, as said below
- wall_normal: float32 [3, 128, 32, 128], P(None, 'tile', 'body'), may hold values from -4 to 4
- wall_arm: float32 [3, 128, 32, 128], P(None, 'tile', 'body'), may hold values from -4 to 4
- wall_live: int32 [128, 32, 128], P('tile', 'body'), may hold values 0 or 1
- wall_body: int32 [128, 32, 128], P('tile', 'body'), may hold values from 0 to 30719, as said below
- linear_velocity: float32 [3, 30720], P(None, 'body'), may hold values from -6 to 6
- angular_velocity: float32 [3, 30720], P(None, 'body'), may hold values from -6 to 6
- inverse_mass: float32 [30720], P('body'), may hold values from 0.2 to 2
- inverse_inertia: float32 [3, 30720], P(None, 'body'), may hold values from 0.2 to 2
Outputs:
- pressure: float32 [128, 32, 128], P('tile', 'body')
- wall_pressure: float32 [128, 32, 128], P('tile', 'body')
- body_state: float32 [6, 30720], P(None, 'body')
- wall_velocity: float32 [3, 128, 32, 128], P(None, 'tile', 'body')
- density_error: float32 [], replicated
Inputs may be any that keep to these rules, and one draw needn't show every extreme that they name: `neighbours`: entry 0 of every list is 4, the block itself; the other entries are distinct codes of the eight blocks around it. `fluid_position`: A particle of block (a, b) has its first coordinate in [a, a + 1), its second in [b, b + 1), its third in [0, 1). `wall_position`: A particle of block (a, b) has its first coordinate in [a, a + 1], its second in [b, b + 1], its third in [0, 1]. `wall_body`: bodies are compact: a boundary particle belongs to a body whose centre lies within a few blocks of its own block.
All inputs are finite; a program needn't handle non-finite values. No bound on the sum of `wall_live` on one device may be relied on, other than what follows from the above.
Results may differ from a plain program's by a relative error of at most 0.0003.
Values sent between devices are 32-bit elements; how exact they have to be, the bound alone decides.
A program may use at most 128 MiB of HBM per device.

v0:
```python
import jax
import jax.numpy as jnp
from jax import lax
from jax.sharding import PartitionSpec as P

SWEEPS = 2
BODIES = 30720


relax_factor = 0.5
inv_width = 2.0
kernel_scale = 0.0078125
wall_offset = 0.5
time_step = 0.25
gravity_z = -9.81


def padded(block, sides, width):
    for axis, dim in sides:
        count = lax.axis_size(axis)
        forward = [(i, i + 1) for i in range(count - 1)]
        backward = [(target, source) for source, target in forward]
        low = lax.ppermute(
            lax.slice_in_dim(block, block.shape[dim] - width, None, axis=dim), axis, forward
        )
        high = lax.ppermute(lax.slice_in_dim(block, 0, width, axis=dim), axis, backward)
        block = jnp.concatenate([low, block, high], axis=dim)
    return block


def pair_sums(padded_pos, padded_val, own_pos, neighbours):
    row_count = own_pos.shape[1]
    columns = own_pos.shape[2]

    def one_row(row_index):
        window_pos = lax.dynamic_slice_in_dim(padded_pos, row_index, 3, 1)
        window_val = lax.dynamic_slice_in_dim(padded_val, row_index, 3, 0)
        shifted_pos = jnp.stack(
            [window_pos[:, i, j : j + columns] for i in range(3) for j in range(3)], 0
        )
        shifted_val = jnp.stack(
            [window_val[i, j : j + columns] for i in range(3) for j in range(3)], 0
        )
        code_list = lax.dynamic_index_in_dim(neighbours, row_index, 0, keepdims=False)
        near_pos = jnp.take_along_axis(
            jnp.transpose(shifted_pos, (2, 0, 1, 3)), code_list[:, :, None, None], axis=1
        )
        near_val = jnp.take_along_axis(
            jnp.transpose(shifted_val, (1, 0, 2)), code_list[:, :, None], axis=1
        )
        own_rows = lax.dynamic_index_in_dim(own_pos, row_index, 1, keepdims=False)
        distance = None
        for component in range(3):
            offset = (
                own_rows[component][:, None, :, None] - near_pos[:, :, component][:, :, None, :]
            )
            distance = offset * offset if distance is None else distance + offset * offset
        weight = jnp.exp(-distance * inv_width) * kernel_scale
        weight_sum = jnp.sum(weight, axis=(1, 3))
        weighted = jnp.einsum("ckij,ckj->ci", weight, near_val, precision=lax.Precision.HIGHEST)
        return (weight_sum, weighted)

    return lax.map(one_row, jnp.arange(row_count, dtype=jnp.int32))


def cross_product(left, right):
    return jnp.stack(
        [
            left[1] * right[2] - left[2] * right[1],
            left[2] * right[0] - left[0] * right[2],
            left[0] * right[1] - left[1] * right[0],
        ],
        0,
    )


def advance(params, totals):
    lift = jnp.array([0.0, 0.0, time_step * gravity_z], dtype=jnp.float32)[:, None]
    linear = params[0:3] + time_step * (params[6][None] * totals[0:3]) + lift
    angular = params[3:6] + time_step * params[7:10] * totals[3:6]
    return jnp.concatenate([linear, angular], 0)


def widened(values):
    return padded(values, (("tile", 0), ("body", 1)), 1)


def shards(
    fluid_position,
    fluid_pressure,
    source,
    stiffness,
    neighbours,
    wall_position,
    wall_normal,
    wall_arm,
    wall_live,
    wall_body,
    linear_velocity,
    angular_velocity,
    inverse_mass,
    inverse_inertia,
):
    padded_pos = padded(fluid_position, (("tile", 1), ("body", 2)), 1)
    pressure = fluid_pressure
    residual = source
    for sweep_index in range(SWEEPS):
        weight_sum, weighted = pair_sums(padded_pos, widened(pressure), fluid_position, neighbours)
        diagonal = stiffness + weight_sum
        residual = source - (diagonal * pressure - weighted)
        pressure = jnp.maximum(pressure + relax_factor * residual / diagonal, 0.0)
    particle_total = residual.size * lax.axis_size("tile") * lax.axis_size("body")
    error_local = jnp.sum(residual * residual) / particle_total
    weight_sum, weighted = pair_sums(padded_pos, widened(pressure), wall_position, neighbours)
    wall_pressure = weighted / (wall_offset + weight_sum) * wall_live.astype(jnp.float32)
    force = wall_pressure[None] * wall_normal
    torque = cross_product(wall_arm, force)
    stacked = jnp.concatenate([force, torque], 0).reshape(6, -1).T
    partials = jax.ops.segment_sum(stacked, wall_body.reshape(-1), num_segments=BODIES).T
    owned = BODIES // lax.axis_size("body")
    first_owned = lax.axis_index("body") * owned
    own_params = jnp.concatenate(
        [linear_velocity, angular_velocity, inverse_mass[None], inverse_inertia], 0
    )
    totals, density_error = lax.psum((partials, error_local), ("tile", "body"))
    all_params = lax.all_gather(own_params, "body", axis=1, tiled=True)
    full_state = advance(all_params, totals)
    own_state = lax.dynamic_slice_in_dim(full_state, first_owned, owned, 1)
    index_flat = wall_body.reshape(-1)
    moving = jnp.take(full_state[0:3], index_flat, axis=1).reshape(wall_arm.shape)
    turning = jnp.take(full_state[3:6], index_flat, axis=1).reshape(wall_arm.shape)
    wall_velocity = moving + cross_product(turning, wall_arm)
    return (pressure, wall_pressure, own_state, wall_velocity, density_error)


def solution(mesh):
    placed = (
        P(None, "tile", "body", None),
        P("tile", "body", None),
        P("tile", "body", None),
        P("tile", "body", None),
        P("tile", "body", None),
        P(None, "tile", "body", None),
        P(None, "tile", "body", None),
        P(None, "tile", "body", None),
        P("tile", "body", None),
        P("tile", "body", None),
        P(None, "body"),
        P(None, "body"),
        P("body"),
        P(None, "body"),
    )
    return jax.shard_map(
        shards,
        mesh=mesh,
        in_specs=placed,
        out_specs=(
            P("tile", "body", None),
            P("tile", "body", None),
            P(None, "body"),
            P(None, "tile", "body", None),
            P(),
        ),
        check_vma=False,
    )
```

profile of v0, /device:TPU:0, one launch (start us, length us, event | category | flops | bytes accessed | tf_op | source)
XLA Modules:
  0.0 1128.1 jit_solution(10268399384290714096)
XLA Ops:
  13.8 4.5 collective-permute-start
  27.3 4.5 collective-permute-start.2
  33.4 4.2 collective-permute-done.3
  37.9 214.2 %while.36 = (s32[]{:T(128)}, f32[16,8,128]{2,1,0:T(8,128)S(1)}, f32[16,8,128]{2,1,0:T(8,128)S(1)}, s32[16]{0:T(128)S(1)}, f32[3,16,8,128]{3,2,1,0:T(8,128)}, /*i...) while((s32[]{:T(128)}, f32[16,8,128]{2,1,0:T(8,128)S(1)}, ...), condition=%wide.region_2.0_spmd, body=%wide.region_0.4_spmd.sunk | while | flops 27549932 | bytes 1204188 | solution.py:63
  254.7 5.0 collective-permute-done.9
  264.7 4.0 collective-permute-done.11
  268.9 214.2 %while.37 = (s32[]{:T(128)}, f32[16,8,128]{2,1,0:T(8,128)S(1)}, f32[16,8,128]{2,1,0:T(8,128)S(1)}, s32[16]{0:T(128)S(1)}, f32[3,16,8,128]{3,2,1,0:T(8,128)}, /*i...) while((s32[]{:T(128)}, f32[16,8,128]{2,1,0:T(8,128)S(1)}, ...), condition=%wide.region_5.8_spmd, body=%wide.region_3.7_spmd.sunk | while | flops 27549932 | bytes 1204188 | solution.py:63
  278.2 4.0 fusion.85
  291.6 4.0 fusion.85
  305.0 4.0 fusion.85
  318.4 4.0 fusion.85
  331.8 4.0 fusion.85
  345.1 4.0 fusion.85
  358.5 4.0 fusion.85
  385.3 4.0 fusion.85
  398.7 4.0 fusion.85
  412.1 4.0 fusion.85
  465.6 4.0 fusion.85
  479.0 4.0 fusion.85
  500.0 214.1 %while.38 = (s32[]{:T(128)}, f32[16,8,128]{2,1,0:T(8,128)S(1)}, f32[16,8,128]{2,1,0:T(8,128)S(1)}, s32[16]{0:T(128)S(1)}, f32[3,16,8,128]{3,2,1,0:T(8,128)}, /*i...) while((s32[]{:T(128)}, f32[16,8,128]{2,1,0:T(8,128)S(1)}, ...), condition=%wide.region_8.11_spmd, body=%wide.region_6.10_spmd.sunk | while | flops 27549932 | bytes 1204188 | solution.py:63
  714.7 5.3 copy.268
  719.9 94.0 %scatter_custom_fusion = f32[30720,6]{1,0:T(8,128)} fusion(s32[16384]{0:T(1024)S(1)} %bitcast.478, f32[16384,6]{1,0:T(8,128)} %copy.268, f32[]{:T(128)} %constant.113.clone.1), kind=kCustom, calls=%fused_computation.226 | custom fusion | flops 98304 | bytes 737792 | tf_op jit(solution)/shard_map/scatter-add | solution.py:119
  814.0 9.5 copy.269
  824.2 41.4 %psum.15 = f32[]{:T(128)} all-reduce(f32[]{:T(128)S(6)} %div.15), channel_id=1, replica_groups=mesh['tile'=8,'body'=4] {'tile','body'}, use_global_device_ids=true, to_apply=%region_12.16 | all-reduce | flops 1 | bytes 8 | tf_op jit(solution)/shard_map/psum | solution.py:125
  866.9 86.7 %all-reduce.2.cloned.1.call-done = f32[6,30720]{1,0:T(8,128)} async-done(((f32[6,30720]{1,0:T(8,128)}), f32[6,30720]{1,0:T(8,128)}) %all-reduce.2.cloned.1.call-update) | async-done | bytes 737296 | tf_op jit(solution)/shard_map/psum | solution.py:125
  956.9 7.7 copy.271
  964.7 7.7 copy.270
  973.2 59.8 %gather_fusion.7 = f32[16384,3]{1,0:T(8,128)} fusion(f32[3,30720]{0,1:T(8,128)} %copy.271, s32[16384]{0:T(1024)S(1)} %fusion.58), kind=kCustom, calls=%fused_computation.7.clone | custom fusion | bytes 458752 | tf_op jit(solution)/shard_map/jit(_take)/gather | solution.py:131
  1033.1 59.9 %gather_fusion.6 = f32[16384,3]{1,0:T(8,128)} fusion(f32[3,30720]{0,1:T(8,128)} %copy.270, s32[16384]{0:T(1024)S(1)} %fusion.58), kind=kCustom, calls=%fused_computation.2.clone | custom fusion | bytes 458752 | tf_op jit(solution)/shard_map/jit(_take)/gather | solution.py:130
  1092.9 10.8 select_bitcast_fusion.3
  1103.7 11.0 slice_reduce_fusion.1
  1114.7 5.2 copy.272
  (1919 shorter events, 479.1 us)
Async XLA Ops:
  8.0 857.6 %all-gather.2.cloned.1.call-start = ((), (), s32[]{:S(2)}) async-start(), calls=%async_computation | async-start | bytes 2457600 | tf_op jit(solution)/shard_map/all_gather | solution.py:126
  8.8 12.5 %collective-permute-start.5 = (f32[1,8,128]{2,1,0:T(8,128)S(1)}, f32[1,8,128]{2,1,0:T(8,128)S(1)}, u32[]{:S(2)}, u32[]{:S(2)}) collective-permute-start(f32[1,8,128]{2,1,0:T(8,128)S(1)} %get-tuple-element.378), channel_id=1, source_target_pairs={{4,0},{8,4},{12,8},{16,12},{20,16},{24,20},{28,24},{5,1},{9,5},{13... | collective-permute-start | bytes 12296 | tf_op jit(solution)/shard_map/ppermute | solution.py:26
  10.0 10.4 collective-permute-start.4
  13.8 12.3 %collective-permute-start = (f32[3,1,8,128]{3,0,2,1:T(4,128)S(1)}, f32[3,1,8,128]{3,0,2,1:T(4,128)S(1)}, u32[]{:S(2)}, u32[]{:S(2)}) collective-permute-start(f32[3,1,8,128]{3,0,2,1:T(4,128)S(1)} %copy.294), channel_id=1, source_target_pairs={{0,4},{4,8},{8,12},{12,16},{16,20},{20,24},{24,28},{1,5},{5,9},{9,... | collective-permute-start | bytes 36872 | tf_op jit(solution)/shard_map/ppermute | solution.py:23
  18.3 8.9 collective-permute-start.1
  21.3 11.8 %collective-permute-start.6 = (f32[18,1,128]{2,1,0:T(1,128)S(1)}, f32[18,1,128]{2,1,0:T(1,128)S(1)}, u32[]{:S(2)}, u32[]{:S(2)}) collective-permute-start(f32[18,1,128]{2,1,0:T(1,128)S(1)} %get-tuple-element.372), channel_id=1, source_target_pairs={{0,1},{1,2},{2,3},{4,5},{5,6},{6,7},{8,9},{9,10},{10,11},{12,13},{... | collective-permute-start | bytes 27656 | tf_op jit(solution)/shard_map/ppermute | solution.py:23
  24.8 8.3 collective-permute-start.7
  27.3 6.2 collective-permute-start.2
  31.8 5.9 collective-permute-start.3
  37.8 214.2 %copy-start.4 = (f32[16,8,128]{2,1,0:T(8,128)S(1)}, f32[16,8,128]{2,1,0:T(8,128)}, u32[]{:S(2)}) copy-start(f32[16,8,128]{2,1,0:T(8,128)} %param.28) | copy-start | bytes 196612
  37.8 214.2 %copy-start.6 = (f32[16,8,128]{2,1,0:T(8,128)S(1)}, f32[16,8,128]{2,1,0:T(8,128)}, u32[]{:S(2)}) copy-start(f32[16,8,128]{2,1,0:T(8,128)} %param.29) | copy-start | bytes 196612
  37.8 214.2 %copy-start.7 = (f32[16,8,128]{2,1,0:T(8,128)S(1)}, f32[16,8,128]{2,1,0:T(8,128)}, u32[]{:S(2)}) copy-start(f32[16,8,128]{2,1,0:T(8,128)} %param.30) | copy-start | bytes 196612
  37.8 226.8 %copy-start.12 = (f32[7680]{0:T(1024)S(1)}, f32[7680]{0:T(1024)}, u32[]{:S(2)}) copy-start(f32[7680]{0:T(1024)} %param.39) | copy-start | bytes 92164
  252.1 2.6 collective-permute-start.8
  253.4 6.3 collective-permute-start.9
  259.7 5.0 collective-permute-start.10
  263.2 5.6 collective-permute-start.11
  268.8 219.0 %copy-start.8 = (f32[3,7680]{1,0:T(4,128)S(1)}, f32[3,7680]{1,0:T(4,128)}, u32[]{:S(2)}) copy-start(f32[3,7680]{1,0:T(4,128)} %param.40) | copy-start | bytes 276484
  268.8 219.0 %copy-start.9 = (f32[3,7680]{1,0:T(4,128)S(1)}, f32[3,7680]{1,0:T(4,128)}, u32[]{:S(2)}) copy-start(f32[3,7680]{1,0:T(4,128)} %param.38) | copy-start | bytes 276484
  268.8 219.0 %copy-start.10 = (f32[3,7680]{1,0:T(4,128)S(1)}, f32[3,7680]{1,0:T(4,128)}, u32[]{:S(2)}) copy-start(f32[3,7680]{1,0:T(4,128)} %param.37) | copy-start | bytes 276484
  268.9 227.0 %copy-start.5 = (s32[16,8,128]{2,1,0:T(8,128)S(1)}, s32[16,8,128]{2,1,0:T(8,128)}, u32[]{:S(2)}) copy-start(s32[16,8,128]{2,1,0:T(8,128)} %param.36) | copy-start | bytes 196612
  483.7 16.3 %copy-start.2 = (f32[16,8,128]{2,1,0:T(8,128)}, f32[16,8,128]{2,1,0:T(8,128)S(1)}, u32[]{:S(2)}) copy-start(f32[16,8,128]{2,1,0:T(8,128)S(1)} %get-tuple-element.360) | copy-start | bytes 196612
  483.7 5.2 collective-permute-start.12
  486.5 4.3 collective-permute-start.13
  488.8 464.7 %all-reduce.2.cloned.1.call-start = ((), (), s32[]{:S(2)}) async-start(), calls=%async_computation.1 | async-start | bytes 1966080 | tf_op jit(solution)/shard_map/psum | solution.py:125
  490.8 5.0 collective-permute-start.14
  494.3 5.6 collective-permute-start.15
  499.9 214.2 %copy-start.11 = (s32[16,8,128]{2,1,0:T(8,128)S(1)}, s32[16,8,128]{2,1,0:T(8,128)}, u32[]{:S(2)}) copy-start(s32[16,8,128]{2,1,0:T(8,128)} %param.35) | copy-start | bytes 196612
  499.9 214.2 %copy-start = (f32[3,16,8,128]{3,2,1,0:T(8,128)S(1)}, f32[3,16,8,128]{3,2,1,0:T(8,128)}, u32[]{:S(2)}) copy-start(f32[3,16,8,128]{3,2,1,0:T(8,128)} %param.33) | copy-start | bytes 589828
  499.9 214.3 %copy-start.1 = (f32[3,16,8,128]{3,2,1,0:T(8,128)S(1)}, f32[3,16,8,128]{3,2,1,0:T(8,128)}, u32[]{:S(2)}) copy-start(f32[3,16,8,128]{3,2,1,0:T(8,128)} %param.34) | copy-start | bytes 589828
  714.2 5.8 copy-start.3
  814.0 139.6 %copy-start.13 = (f32[3]{0:T(128)S(1)}, f32[3]{0:T(128)}, u32[]{:S(2)}) copy-start(f32[3]{0:T(128)} %constant.120.clone) | copy-start | bytes 40
Sparse Core Ops, SparseCore 0:
  488.9 46.8 all-gather.1
Sparse Core Ops, SparseCore 1:
  823.6 129.9 all-reduce.1
where the time goes:
time: 1130 us
  local copies, waits for them, and re-layouts  359 us (32%)
  other arithmetic  212 us (19%)
  matrix products  193 us (17%)
  loops' own time  163 us (14%)
  waiting for transfers between devices  106 us (9%)
  blocking collectives  41.4 us (4%)
  starting transfers between devices  37.4 us (3%)
  between operations  16.7 us (1%)
    dot_general x48, matrix products, one_row(): jnp.einsum('ckij,ckj->ci', weight, near_val, precision=lax.Precision.HIGH...  193 us
    another operation x3, loops' own time, pair_sums(): return lax.map(one_row, jnp.arange(row_count, dtype=jnp.int32))  163 us
    scatter-add x1, other arithmetic, shards(): jax.ops.segment_sum(stacked, wall_body.reshape(-1), num_segments=BODIES)  94 us
    reduce_sum x48, other arithmetic, one_row(): weight_sum = jnp.sum(weight, axis=(1, 3))  90.2 us
    psum x1, waiting for transfers between devices, shards(): totals, density_error = lax.psum((partials, error_local), ('tile', 'body'))  86.7 us
    gather x1, local copies, waits for them, and re-layouts, shards(): jnp.take(full_state[0:3], index_flat, axis=1).reshape(wall_arm.shape)  59.9 us
    gather x1, local copies, waits for them, and re-layouts, shards(): jnp.take(full_state[3:6], index_flat, axis=1).reshape(wall_arm.shape)  59.8 us
    gather x144, local copies, waits for them, and re-layouts, one_row(): jnp.take_along_axis(jnp.transpose(shifted_pos, (2, 0, 1, 3)), code_list[:...  53 us
  transfers between devices with their start and end apart: 18, of which 7 were waited for; matrix products, arithmetic and copies ran while one was open for 24% of the time, Pallas kernels for 0%

commit v1 on v0

v1 whole, which is shorter than its diff:
```python
import math
import functools
import jax
import jax.numpy as jnp
from jax import lax
from jax.experimental import pallas as pl
from jax.experimental.pallas import tpu as pltpu
from jax.sharding import PartitionSpec as P

SWEEPS = 2

relax_factor = 0.5
inv_width = 2.0
kernel_scale = 0.0078125
wall_offset = 0.5
time_step = 0.25
gravity_z = -9.81

UNIT = math.sqrt(inv_width / math.log(2.0))
DEPTH = 32
LOW = 256
F32, BF16 = jnp.float32, jnp.bfloat16
VMEM = pltpu.VMEM
SMEM = pltpu.SMEM


def padded(block, sides, width):
    for axis, dim in sides:
        count = lax.axis_size(axis)
        forward = [(i, i + 1) for i in range(count - 1)]
        backward = [(target, source) for source, target in forward]
        low = lax.ppermute(
            lax.slice_in_dim(block, block.shape[dim] - width, None, axis=dim), axis, forward
        )
        high = lax.ppermute(lax.slice_in_dim(block, 0, width, axis=dim), axis, backward)
        block = jnp.concatenate([low, block, high], axis=dim)
    return block


def pieces(x, count):
    out = []
    for _ in range(count):
        piece = x.astype(BF16).astype(F32)
        out.append(piece)
        x = x - piece
    return out


def own_features(x, y, z):
    rows = []
    for coordinate in (x, y, z):
        h, m, l = pieces(2.0 * coordinate, 3)
        rows += [h, h, m, m, h, l]
    rows += pieces(-(x * x + y * y + z * z), 3)
    one = jnp.ones_like(x)
    return rows + [one, one, one]


def near_features(x, y, z):
    rows = []
    for coordinate in (x, y, z):
        h, m, l = pieces(coordinate, 3)
        rows += [h, m, h, m, l, h]
    one = jnp.ones_like(x)
    rows += [one, one, one]
    return rows + pieces(-(x * x + y * y + z * z), 3)


def column_base(shape, first):
    return (first + lax.broadcasted_iota(jnp.int32, shape, 0)).astype(F32) + 0.5


def build_near(pos_ref, base_ref, fj_ref, stage_ref, cols):
    rows, wide = pos_ref.shape[1], pos_ref.shape[2]
    stage_ref[...] = jnp.zeros_like(stage_ref)

    def row(r, carry):
        x = (pos_ref[0, r] - ((base_ref[0] + r - 1).astype(F32) + 0.5)) * UNIT
        y = (pos_ref[1, r] - column_base((wide, 128), base_ref[1] - 1)) * UNIT
        z = (pos_ref[2, r] - 0.5) * UNIT
        for k, value in enumerate(near_features(x, y, z)):
            stage_ref[k * wide : (k + 1) * wide] = value
        for c in range(cols + 2):
            features = stage_ref[pl.ds(c, DEPTH, stride=wide), :]
            start = pl.multiple_of((r * (cols + 2) + c) * 128, 128)
            fj_ref[pl.ds(start, 128), 0:DEPTH] = features.T.astype(BF16)
        return carry

    lax.fori_loop(0, rows, row, 0)


def build_values(val_ref, pb_ref, cols):
    def row(r, carry):
        turned = val_ref[r].T
        for c in range(cols + 2):
            start = pl.multiple_of((r * (cols + 2) + c) * 128, 128)
            pb_ref[pl.ds(start, 128), :] = jnp.broadcast_to(turned[:, c : c + 1], (128, 128))
        return carry

    lax.fori_loop(0, val_ref.shape[0], row, 0)


def pair_row(r, own, base_ref, near_ref, fj_ref, pb_ref, si_ref, ws_ref, wv_ref, cols):
    x = (own[0] - ((base_ref[0] + r).astype(F32) + 0.5)) * UNIT
    y = (own[1] - column_base((cols, 128), base_ref[1])) * UNIT
    z = (own[2] - 0.5) * UNIT
    for q in range(9):
        shifted = own_features(x - (q // 3 - 1) * UNIT, y - (q % 3 - 1) * UNIT, z)
        for k, value in enumerate(shifted):
            at = (q * DEPTH + k) * cols
            si_ref[at : at + cols] = value
    listed = near_ref.shape[2]
    for c in range(cols):
        ws = jnp.zeros((8, 128), F32)
        wv = jnp.zeros((8, 128), F32)
        for k in range(listed):
            code = near_ref[r, c, k]
            up = code // 3
            block = (r + up) * (cols + 2) + c + code - up * 3
            start = pl.multiple_of(block * 128, 128)
            features = si_ref[pl.ds(code * (DEPTH * cols) + c, DEPTH, stride=cols), :]
            exponent = jnp.dot(
                fj_ref[pl.ds(start, 128), 0:DEPTH],
                features.astype(BF16),
                preferred_element_type=F32,
            )
            weight = jnp.exp2(exponent)
            product = weight * pb_ref[pl.ds(start, 128), :]
            ws = ws + jnp.sum(weight.reshape(16, 8, 128), axis=0)
            wv = wv + jnp.sum(product.reshape(16, 8, 128), axis=0)
        ws_ref[r, c : c + 1] = jnp.sum(ws, axis=0, keepdims=True) * kernel_scale
        wv_ref[r, c : c + 1] = jnp.sum(wv, axis=0, keepdims=True) * kernel_scale


def sweep_kernel(
    first, base_ref, near_ref, pos_ref, own_ref, val_ref, p_ref, source_ref, stiff_ref, *rest
):
    if first:
        p_out, fj_ref, pb_ref, si_ref, ws_ref, wv_ref, stage_ref = rest
    else:
        fj_ref, p_out, error_ref, pb_ref, si_ref, ws_ref, wv_ref = rest
    rows, cols = p_ref.shape[0], p_ref.shape[1]
    if first:
        for c0 in range(0, si_ref.shape[0], 1024):
            pass
        build_near(pos_ref, base_ref, fj_ref, stage_ref, cols)
    si_ref[...] = jnp.zeros_like(si_ref)
    build_values(val_ref, pb_ref, cols)

    def row(r, carry):
        own = [own_ref[d, r] for d in range(3)]
        pair_row(r, own, base_ref, near_ref, fj_ref, pb_ref, si_ref, ws_ref, wv_ref, cols)
        return carry

    lax.fori_loop(0, rows, row, 0)
    pressure = p_ref[...]
    diagonal = stiff_ref[...] + ws_ref[...]
    residual = source_ref[...] - (diagonal * pressure - wv_ref[...])
    p_out[...] = jnp.maximum(pressure + relax_factor * residual / diagonal, 0.0)
    if not first:
        error_ref[...] = jnp.sum(residual * residual, axis=0)


def wall_kernel(
    base_ref, near_ref, own_ref, val_ref, live_ref, fj_ref, out_ref, pb_ref, si_ref, ws_ref, wv_ref
):
    rows, cols = out_ref.shape[0], out_ref.shape[1]
    si_ref[...] = jnp.zeros_like(si_ref)
    build_values(val_ref, pb_ref, cols)

    def row(r, carry):
        own = [own_ref[d, r] for d in range(3)]
        pair_row(r, own, base_ref, near_ref, fj_ref, pb_ref, si_ref, ws_ref, wv_ref, cols)
        return carry

    lax.fori_loop(0, rows, row, 0)
    out_ref[...] = wv_ref[...] / (wall_offset + ws_ref[...]) * live_ref[...].astype(F32)


def scatter_kernel(high, wp_ref, normal_ref, arm_ref, body_ref, out_ref, val_ref, lhs_ref, rhs_ref):
    rows, cols = wp_ref.shape[0], wp_ref.shape[1]
    out_ref[...] = jnp.zeros_like(out_ref)
    high_iota = lax.broadcasted_iota(jnp.int32, (high, 128), 0)
    low_iota = lax.broadcasted_iota(jnp.int32, (LOW, 128), 0)

    def row(r, carry):
        wp = wp_ref[r]
        fx, fy, fz = [wp * normal_ref[d, r] for d in range(3)]
        ax, ay, az = [arm_ref[d, r] for d in range(3)]
        values = [fx, fy, fz, ay * fz - az * fy, az * fx - ax * fz, ax * fy - ay * fx]
        for q, value in enumerate(values):
            for s, piece in enumerate(pieces(value, 2)):
                val_ref[q * 2 + s] = piece
        body = body_ref[r]
        for c in range(cols):
            line = body[c : c + 1]
            top = line // LOW
            at_high = high_iota == top
            at_low = (low_iota == line - top * LOW).astype(F32).astype(BF16)
            for s in range(2):
                lanes = slice((c * 2 + s) * 128, (c * 2 + s + 1) * 128)
                rhs_ref[:, lanes] = at_low
                for q in range(6):
                    value = val_ref[q * 2 + s, c : c + 1]
                    lhs_ref[q * high : (q + 1) * high, lanes] = jnp.where(
                        at_high, value, 0.0
                    ).astype(BF16)
        out_ref[...] += lax.dot_general(
            lhs_ref[...], rhs_ref[...], (((1,), (1,)), ((), ())), preferred_element_type=F32
        )
        return carry

    lax.fori_loop(0, rows, row, 0)


def gather_kernel(high, state_ref, arm_ref, body_ref, out_ref, lhs_ref, got_ref):
    rows, cols = body_ref.shape[0], body_ref.shape[1]
    for q in range(6):
        for s, piece in enumerate(pieces(state_ref[q], 2)):
            lhs_ref[q * LOW : (q + 1) * LOW, s * high : (s + 1) * high] = piece.T.astype(BF16)
    high_iota = lax.broadcasted_iota(jnp.int32, (high, 256), 0)
    low_iota = lax.broadcasted_iota(jnp.int32, (LOW, 256), 0)

    def row(r, carry):
        body = body_ref[r]
        for c in range(0, cols, 2):
            line = jnp.concatenate([body[c : c + 1], body[c + 1 : c + 2]], axis=1)
            top = line // LOW
            at_high = (high_iota == top).astype(F32).astype(BF16)
            at_low = low_iota == line - top * LOW
            rhs = jnp.concatenate([at_high, at_high], axis=0)
            for q in range(6):
                found = jnp.dot(
                    lhs_ref[q * LOW : (q + 1) * LOW], rhs, preferred_element_type=F32
                )
                line_q = jnp.sum(jnp.where(at_low, found, 0.0), axis=0, keepdims=True)
                got_ref[q, r, c : c + 1] = line_q[:, :128]
                got_ref[q, r, c + 1 : c + 2] = line_q[:, 128:]
        return carry

    lax.fori_loop(0, rows, row, 0)
    ax, ay, az = arm_ref[0], arm_ref[1], arm_ref[2]
    vx, vy, vz, wx, wy, wz = [got_ref[q] for q in range(6)]
    out_ref[0] = vx + (wy * az - wz * ay)
    out_ref[1] = vy + (wz * ax - wx * az)
    out_ref[2] = vz + (wx * ay - wy * ax)


def call(kernel, shapes, ins, scratch, spaces, name):
    return pl.pallas_call(
        kernel,
        out_shape=shapes,
        in_specs=[pl.BlockSpec(memory_space=s) for s in spaces],
        out_specs=jax.tree.map(lambda _: pl.BlockSpec(memory_space=VMEM), shapes),
        scratch_shapes=scratch,
        compiler_params=pltpu.CompilerParams(vmem_limit_bytes=60 * 2**20),
        name=name,
    )(*ins)


def shape(dims, kind=F32):
    return jax.ShapeDtypeStruct(tuple(dims), kind)


def wide_columns(block):
    extra = -block.shape[-2] % 8
    widths = [(0, 0)] * block.ndim
    widths[-2] = (0, extra)
    return jnp.pad(block, widths)


def advance(params, totals):
    lift = jnp.array([0.0, 0.0, time_step * gravity_z], dtype=F32)[:, None, None]
    linear = params[0:3] + time_step * (params[6][None] * totals[0:3]) + lift
    angular = params[3:6] + time_step * params[7:10] * totals[3:6]
    return jnp.concatenate([linear, angular], 0)


def widened(values):
    return wide_columns(padded(values, (("tile", 0), ("body", 1)), 1))


def shards(
    fluid_position,
    fluid_pressure,
    source,
    stiffness,
    neighbours,
    wall_position,
    wall_normal,
    wall_arm,
    wall_live,
    wall_body,
    linear_velocity,
    angular_velocity,
    inverse_mass,
    inverse_inertia,
):
    rows, cols, _ = fluid_pressure.shape
    blocks = (rows + 2) * (cols + 2)
    base = jnp.stack([lax.axis_index("tile") * rows, lax.axis_index("body") * cols]).astype(jnp.int32)
    both = wide_columns(
        padded(
            jnp.concatenate([fluid_position, fluid_pressure[None]], 0),
            (("tile", 1), ("body", 2)),
            1,
        )
    )
    padded_pos, padded_val = both[:3], both[3]
    wide = padded_pos.shape[2]
    small = shape((rows, cols, 128))
    fj_shape = (blocks * 128, 128)
    pair_scratch = [
        VMEM((blocks * 128, 128), F32),
        VMEM((9 * DEPTH * cols, 128), F32),
        VMEM((rows, cols, 128), F32),
        VMEM((rows, cols, 128), F32),
    ]
    pressure, near = call(
        functools.partial(sweep_kernel, True),
        (small, shape(fj_shape, BF16)),
        (base, neighbours, padded_pos, fluid_position, padded_val, fluid_pressure, source, stiffness),
        pair_scratch + [VMEM((DEPTH * wide, 128), F32)],
        [SMEM] * 2 + [VMEM] * 6,
        "sweep_first",
    )

    def second(base_ref, near_ref, own_ref, val_ref, *rest):
        sweep_kernel(False, base_ref, near_ref, None, own_ref, val_ref, *rest)

    pressure, error = call(
        second,
        (small, shape((cols, 128))),
        (base, neighbours, fluid_position, widened(pressure), pressure, source, stiffness, near),
        pair_scratch,
        [SMEM] * 2 + [VMEM] * 6,
        "sweep_second",
    )
    wall_pressure = call(
        wall_kernel,
        small,
        (base, neighbours, wall_position, widened(pressure), wall_live, near),
        pair_scratch,
        [SMEM] * 2 + [VMEM] * 4,
        "wall",
    )
    particle_total = rows * cols * 128 * lax.axis_size("tile") * lax.axis_size("body")
    error_local = jnp.sum(error) / particle_total

    bodies_own = inverse_mass.shape[0]
    bodies = bodies_own * lax.axis_size("body")
    count = -(-bodies // LOW)
    high = -(-count // 16) * 16
    high = max(high, 128)
    partials = call(
        functools.partial(scatter_kernel, high),
        shape((6 * high, LOW)),
        (wall_pressure, wall_normal, wall_arm, wall_body),
        [
            VMEM((12, cols, 128), F32),
            VMEM((6 * high, cols * 256), BF16),
            VMEM((LOW, cols * 256), BF16),
        ],
        [VMEM] * 4,
        "scatter",
    )
    own_params = jnp.concatenate(
        [linear_velocity, angular_velocity, inverse_mass[None], inverse_inertia], 0
    )
    all_params = lax.all_gather(own_params, "body", axis=1, tiled=True)
    all_params = jnp.pad(all_params, ((0, 0), (0, high * LOW - bodies))).reshape(10, high, LOW)
    totals, density_error = lax.psum((partials, error_local), ("tile", "body"))
    full_state = advance(all_params, totals.reshape(6, high, LOW))
    flat = full_state.reshape(6, high * LOW)
    own_state = lax.dynamic_slice_in_dim(flat, lax.axis_index("body") * bodies_own, bodies_own, 1)
    wall_velocity = call(
        functools.partial(gather_kernel, high),
        shape((3, rows, cols, 128)),
        (full_state, wall_arm, wall_body),
        [VMEM((6 * LOW, 2 * high), BF16), VMEM((6, rows, cols, 128), F32)],
        [VMEM] * 3,
        "gather",
    )
    return (pressure, wall_pressure, own_state, wall_velocity, density_error)


def solution(mesh):
    placed = (
        P(None, "tile", "body", None),
        P("tile", "body", None),
        P("tile", "body", None),
        P("tile", "body", None),
        P("tile", "body", None),
        P(None, "tile", "body", None),
        P(None, "tile", "body", None),
        P(None, "tile", "body", None),
        P("tile", "body", None),
        P("tile", "body", None),
        P(None, "body"),
        P(None, "body"),
        P("body"),
        P(None, "body"),
    )
    return jax.shard_map(
        shards,
        mesh=mesh,
        in_specs=placed,
        out_specs=(
            P("tile", "body", None),
            P("tile", "body", None),
            P(None, "body"),
            P(None, "tile", "body", None),
            P(),
        ),
        check_vma=False,
    )
```

time: 1130 us -> 352 us (0.31)
  local copies, waits for them, and re-layouts: 359 us -> 12.2 us
  other arithmetic: 212 us -> 10.4 us
  matrix products: 193 us -> 0 us
  loops' own time: 163 us -> 0 us
  Pallas kernels: 0 us -> 112 us
  waiting for transfers between devices: 106 us -> 131 us
    gather x338 -> x0, local copies, waits for them, and re-layouts: 220 us -> none  [the longest x1 59.9 us: shards(): jnp.take(full_state[0:3], index_flat, axis=1).reshape(wall_arm.shape)]
    dot_general x48 -> x0, matrix products: 193 us -> none  [one_row(): jnp.einsum('ckij,ckj->ci', weight, near_val, precision=lax.Precision.HIGH...]
    another operation x3 -> x0, loops' own time: 163 us -> none  [pair_sums(): return lax.map(one_row, jnp.arange(row_count, dtype=jnp.int32))]
    pallas_call x0 -> x5, Pallas kernels: none -> 112 us  [call(): pl.pallas_call(kernel, out_shape=shapes, in_specs=[pl.BlockSpec(memory_sp...]
    scatter-add x1 -> x0, other arithmetic: 94 us -> none  [shards(): jax.ops.segment_sum(stacked, wall_body.reshape(-1), num_segments=BODIES)]
    reduce_sum x49 -> x1, other arithmetic: 90.8 us -> 0.6 us  [shards(): error_local = jnp.sum(error) / particle_total]
    sub x96 -> x0, local copies, waits for them, and re-layouts: 35.3 us -> none  [one_row(): own_rows[component][:, None, :, None]]
    dynamic_slice x48 -> x0, local copies, waits for them, and re-layouts: 28.7 us -> none  [pair_sums(): return lax.map(one_row, jnp.arange(row_count, dtype=jnp.int32))]
  transfers between devices with their start and end apart: 18 -> 14, of which waited for: 7 -> 8; matrix products, arithmetic and copies ran while one was open for 24% -> 2% of each run, Pallas kernels for 0% -> 0%
where the time goes in v1:
time: 352 us; the launch traced here: 351 us
  waiting for transfers between devices  131 us (37%)
  Pallas kernels  112 us (32%)
  blocking collectives  42.9 us (12%)
  starting transfers between devices  26.4 us (8%)
  between operations  16.4 us (5%)
  local copies, waits for them, and re-layouts  12.2 us (3%)
  other arithmetic  10.4 us (3%)
    psum x1, waiting for transfers between devices, shards(): totals, density_error = lax.psum((partials, error_local), ('tile', 'body'))  112 us
    pallas_call x5, Pallas kernels, call(): pl.pallas_call(kernel, out_shape=shapes, in_specs=[pl.BlockSpec(memory_sp...  112 us
    psum x1, blocking collectives, shards(): totals, density_error = lax.psum((partials, error_local), ('tile', 'body'))  42.9 us
    ppermute x6, starting transfers between devices, padded(): lax.ppermute(lax.slice_in_dim(block, block.shape[dim] - width, None, axis...  18.6 us
    ppermute x6, waiting for transfers between devices, padded(): lax.ppermute(lax.slice_in_dim(block, 0, width, axis=dim), axis, backward)  18.5 us
    ppermute x6, starting transfers between devices, padded(): lax.ppermute(lax.slice_in_dim(block, 0, width, axis=dim), axis, backward)  7.75 us
  transfers between devices with their start and end apart: 14, of which 8 were waited for; matrix products, arithmetic and copies ran while one was open for 2% of the time, Pallas kernels for 0%

profile of v1, /device:TPU:0, one launch (start us, length us, event | category | flops | bytes accessed | tf_op | source)
XLA Modules:
  0.0 350.6 jit_solution(18434732978132881236)
XLA Ops:
  8.8 2.4 collective-permute-start
  11.2 1.3 collective-permute-start.1
  12.5 3.9 %collective-permute-done.1 = f32[4,1,8,128]{3,2,1,0:T(8,128)S(1)} collective-permute-done((f32[4,1,8,128]{3,2,1,0:T(8,128)S(1)}, f32[4,1,8,128]{3,2,1,0:T(8,128)S(1)}, u32[]{:S(2)}, u32[]{:S(2)}) %collective-permute-start.1) | collective-permute-done | bytes 16416 | tf_op jit(solution)/shard_map/ppermute | solution.py:35
  16.4 1.1 pad_maximum_fusion.5
  17.5 3.5 collective-permute-start.2
  21.0 1.3 collective-permute-start.3
  23.0 1.5 copy.21.near_ref
  24.5 2.4 collective-permute-done.3
  26.9 1.1 select_maximum_fusion
  29.5 27.1 %sweep_first.1 = (f32[16,8,128]{2,1,0:T(8,128)}, bf16[23040,128]{1,0:T(8,128)(2,1)}) custom-call(s32[2]{0:T(128)} %pad_add_fusion.base_ref, s32[16,8,6]{2,1,0:T(8,128)} %copy.21.near_ref, f32[3,18,16,128]{3,2,1,0:T(8,128)} %slice.104.pos_ref, f32[3,16,8,128]{3,2,1,0:T(8,128)} %own_ref.4, f32[18,16,128]{2,1,0:T(8,128)} %slice_bitcast_fusion.val_ref, ...), custom_call_target="tpu_custom_call" | custom-call | tf_op jit(solution)/shard_map/sweep_first/pallas_call | solution.py:250
  57.3 2.9 collective-permute-start.4
  60.2 1.3 collective-permute-start.5
  62.4 1.9 collective-permute-done.5
  64.3 3.5 collective-permute-start.6
  67.8 1.3 collective-permute-start.7
  69.1 4.2 %collective-permute-done.7 = f32[18,1,128]{2,1,0:T(1,128)S(1)} collective-permute-done((f32[18,1,128]{2,1,0:T(1,128)S(1)}, f32[18,1,128]{2,1,0:T(1,128)S(1)}, u32[]{:S(2)}, u32[]{:S(2)}) %collective-permute-start.7) | collective-permute-done | bytes 9248 | tf_op jit(solution)/shard_map/ppermute | solution.py:35
  74.0 22.5 %sweep_second.1 = (f32[16,8,128]{2,1,0:T(8,128)}, f32[8,128]{1,0:T(8,128)}) custom-call(s32[2]{0:T(128)} %pad_add_fusion.base_ref, s32[16,8,6]{2,1,0:T(8,128)} %copy.21.near_ref, f32[3,16,8,128]{3,2,1,0:T(8,128)} %own_ref.4, f32[18,16,128]{2,1,0:T(8,128)} %select_maximum_fusion.4.val_ref, f32[16,8,128]{2,1,0:T(8,128)} %get-tuple-element.9.rest_0_, ...), custom_call_target="tpu_custom_call" | custom-call | tf_op jit(solution)/shard_map/sweep_second/pallas_call | solution.py:250
  97.2 2.8 collective-permute-start.8
  100.0 1.3 collective-permute-start.9
  102.2 2.0 collective-permute-done.9
  104.2 3.5 collective-permute-start.10
  107.7 1.3 collective-permute-start.11
  109.1 4.2 %collective-permute-done.11 = f32[18,1,128]{2,1,0:T(1,128)S(1)} collective-permute-done((f32[18,1,128]{2,1,0:T(1,128)S(1)}, f32[18,1,128]{2,1,0:T(1,128)S(1)}, u32[]{:S(2)}, u32[]{:S(2)}) %collective-permute-start.11) | collective-permute-done | bytes 9248 | tf_op jit(solution)/shard_map/ppermute | solution.py:35
  114.0 22.4 %wall.1.wp_ref = f32[16,8,128]{2,1,0:T(8,128)} custom-call(s32[2]{0:T(128)} %pad_add_fusion.base_ref, s32[16,8,6]{2,1,0:T(8,128)} %copy.21.near_ref, f32[3,16,8,128]{3,2,1,0:T(8,128)} %own_ref.5, f32[18,16,128]{2,1,0:T(8,128)} %select_maximum_fusion.2.val_ref, s32[16,8,128]{2,1,0:T(8,128)} %live_ref.1, bf16[23040,128]{1,0:T(8,128)(2,1)} %get-tuple-element.10.rest_3_.fj_ref), custom_call_target="tpu_custom_call" | custom-call | tf_op jit(solution)/shard_map/wall/pallas_call | solution.py:250
  136.4 20.9 %scatter.1 = f32[768,256]{1,0:T(8,128)} custom-call(f32[16,8,128]{2,1,0:T(8,128)} %wall.1.wp_ref, f32[3,16,8,128]{3,2,1,0:T(8,128)} %normal_ref.1, f32[3,16,8,128]{3,2,1,0:T(8,128)} %arm_ref.3, s32[16,8,128]{2,1,0:T(8,128)} %body_ref.3), custom_call_target="tpu_custom_call" | custom-call | tf_op jit(solution)/shard_map/scatter/pallas_call | solution.py:250
  159.6 42.9 %psum.15 = f32[]{:T(128)} all-reduce(f32[]{:T(128)S(6)} %div.3), channel_id=1, replica_groups=mesh['tile'=8,'body'=4] {'tile','body'}, use_global_device_ids=true, to_apply=%region_2.3 | all-reduce | flops 1 | bytes 8 | tf_op jit(solution)/shard_map/psum | solution.py:372
  202.6 112.1 %all-reduce.6.cloned.1.call-done = f32[768,256]{1,0:T(8,128)} async-done(((f32[768,256]{1,0:T(8,128)}), f32[768,256]{1,0:T(8,128)}) %all-reduce.6.cloned.1.call-update) | async-done | bytes 786448 | tf_op jit(solution)/shard_map/psum | solution.py:372
  314.6 1.2 fusion.12
  316.8 1.0 slice.99
  318.4 2.3 fusion.11
  320.7 1.7 pad_slice_fusion.3
  323.7 18.7 %gather.1 = f32[3,16,8,128]{3,2,1,0:T(8,128)} custom-call(f32[6,128,256]{2,1,0:T(8,128)} %pad_maximum_fusion.state_ref, f32[3,16,8,128]{3,2,1,0:T(8,128)} %arm_ref.3, s32[16,8,128]{2,1,0:T(8,128)} %body_ref.3), custom_call_target="tpu_custom_call" | custom-call | tf_op jit(solution)/shard_map/gather/pallas_call | solution.py:250
  (50 shorter events, 12.9 us)
Async XLA Ops:
  8.0 306.6 %all-reduce.6.cloned.1.call-start = ((), (), s32[]{:S(2)}) async-start(), calls=%async_computation.1 | async-start | bytes 1572864 | tf_op jit(solution)/shard_map/psum | solution.py:372
  8.8 3.7 %collective-permute-start = (f32[4,1,8,128]{3,2,1,0:T(8,128)S(1)}, f32[4,1,8,128]{3,2,1,0:T(8,128)S(1)}, u32[]{:S(2)}, u32[]{:S(2)}) collective-permute-start(f32[4,1,8,128]{3,2,1,0:T(8,128)S(1)} %get-tuple-element.24), channel_id=1, source_target_pairs={{0,4},{4,8},{8,12},{12,16},{16,20},{20,24},{24,28},{1,5},{5,9},{9,... | collective-permute-start | bytes 49160 | tf_op jit(solution)/shard_map/ppermute | solution.py:32
  11.2 5.2 %collective-permute-start.1 = (f32[4,1,8,128]{3,2,1,0:T(8,128)S(1)}, f32[4,1,8,128]{3,2,1,0:T(8,128)S(1)}, u32[]{:S(2)}, u32[]{:S(2)}) collective-permute-start(f32[4,1,8,128]{3,2,1,0:T(8,128)S(1)} %get-tuple-element.25), channel_id=1, source_target_pairs={{4,0},{8,4},{12,8},{16,12},{20,16},{24,20},{28,24},{5,1},{9,5},{13... | collective-permute-start | bytes 49160 | tf_op jit(solution)/shard_map/ppermute | solution.py:35
  17.5 6.9 %collective-permute-start.2 = (f32[4,18,1,128]{3,2,1,0:T(1,128)S(1)}, f32[4,18,1,128]{3,2,1,0:T(1,128)S(1)}, u32[]{:S(2)}, u32[]{:S(2)}) collective-permute-start(f32[4,18,1,128]{3,2,1,0:T(1,128)S(1)} %get-tuple-element.22), channel_id=1, source_target_pairs={{0,1},{1,2},{2,3},{4,5},{5,6},{6,7},{8,9},{9,10},{10,11},{12,13},{... | collective-permute-start | bytes 110600 | tf_op jit(solution)/shard_map/ppermute | solution.py:32
  21.0 5.9 %collective-permute-start.3 = (f32[4,18,1,128]{3,2,1,0:T(1,128)S(1)}, f32[4,18,1,128]{3,2,1,0:T(1,128)S(1)}, u32[]{:S(2)}, u32[]{:S(2)}) collective-permute-start(f32[4,18,1,128]{3,2,1,0:T(1,128)S(1)} %get-tuple-element.23), channel_id=1, source_target_pairs={{1,0},{2,1},{3,2},{5,4},{6,5},{7,6},{9,8},{10,9},{11,10},{13,12},{... | collective-permute-start | bytes 110600 | tf_op jit(solution)/shard_map/ppermute | solution.py:35
  57.3 4.3 %collective-permute-start.4 = (f32[1,8,128]{2,1,0:T(8,128)S(1)}, f32[1,8,128]{2,1,0:T(8,128)S(1)}, u32[]{:S(2)}, u32[]{:S(2)}) collective-permute-start(f32[1,8,128]{2,1,0:T(8,128)S(1)} %get-tuple-element.33), channel_id=1, source_target_pairs={{0,4},{4,8},{8,12},{12,16},{16,20},{20,24},{24,28},{1,5},{5,9},{9,... | collective-permute-start | bytes 12296 | tf_op jit(solution)/shard_map/ppermute | solution.py:32
  60.2 4.0 %collective-permute-start.5 = (f32[1,8,128]{2,1,0:T(8,128)S(1)}, f32[1,8,128]{2,1,0:T(8,128)S(1)}, u32[]{:S(2)}, u32[]{:S(2)}) collective-permute-start(f32[1,8,128]{2,1,0:T(8,128)S(1)} %get-tuple-element.32), channel_id=1, source_target_pairs={{4,0},{8,4},{12,8},{16,12},{20,16},{24,20},{28,24},{5,1},{9,5},{13... | collective-permute-start | bytes 12296 | tf_op jit(solution)/shard_map/ppermute | solution.py:35
  64.3 4.8 %collective-permute-start.6 = (f32[18,1,128]{2,1,0:T(1,128)S(1)}, f32[18,1,128]{2,1,0:T(1,128)S(1)}, u32[]{:S(2)}, u32[]{:S(2)}) collective-permute-start(f32[18,1,128]{2,1,0:T(1,128)S(1)} %get-tuple-element.28), channel_id=1, source_target_pairs={{0,1},{1,2},{2,3},{4,5},{5,6},{6,7},{8,9},{9,10},{10,11},{12,13},{... | collective-permute-start | bytes 27656 | tf_op jit(solution)/shard_map/ppermute | solution.py:32
  67.8 5.6 %collective-permute-start.7 = (f32[18,1,128]{2,1,0:T(1,128)S(1)}, f32[18,1,128]{2,1,0:T(1,128)S(1)}, u32[]{:S(2)}, u32[]{:S(2)}) collective-permute-start(f32[18,1,128]{2,1,0:T(1,128)S(1)} %get-tuple-element.29), channel_id=1, source_target_pairs={{1,0},{2,1},{3,2},{5,4},{6,5},{7,6},{9,8},{10,9},{11,10},{13,12},{... | collective-permute-start | bytes 27656 | tf_op jit(solution)/shard_map/ppermute | solution.py:35
  74.0 35.0 %copy-start.4 = (f32[7680]{0:T(1024)S(1)}, f32[7680]{0:T(1024)}, u32[]{:S(2)}) copy-start(f32[7680]{0:T(1024)} %param.27) | copy-start | bytes 92164
  97.2 4.1 %collective-permute-start.8 = (f32[1,8,128]{2,1,0:T(8,128)S(1)}, f32[1,8,128]{2,1,0:T(8,128)S(1)}, u32[]{:S(2)}, u32[]{:S(2)}) collective-permute-start(f32[1,8,128]{2,1,0:T(8,128)S(1)} %get-tuple-element.31), channel_id=1, source_target_pairs={{0,4},{4,8},{8,12},{12,16},{16,20},{20,24},{24,28},{1,5},{5,9},{9,... | collective-permute-start | bytes 12296 | tf_op jit(solution)/shard_map/ppermute | solution.py:32
  100.0 4.2 %collective-permute-start.9 = (f32[1,8,128]{2,1,0:T(8,128)S(1)}, f32[1,8,128]{2,1,0:T(8,128)S(1)}, u32[]{:S(2)}, u32[]{:S(2)}) collective-permute-start(f32[1,8,128]{2,1,0:T(8,128)S(1)} %get-tuple-element.30), channel_id=1, source_target_pairs={{4,0},{8,4},{12,8},{16,12},{20,16},{24,20},{28,24},{5,1},{9,5},{13... | collective-permute-start | bytes 12296 | tf_op jit(solution)/shard_map/ppermute | solution.py:35
  104.2 4.8 %collective-permute-start.10 = (f32[18,1,128]{2,1,0:T(1,128)S(1)}, f32[18,1,128]{2,1,0:T(1,128)S(1)}, u32[]{:S(2)}, u32[]{:S(2)}) collective-permute-start(f32[18,1,128]{2,1,0:T(1,128)S(1)} %get-tuple-element.26), channel_id=1, source_target_pairs={{0,1},{1,2},{2,3},{4,5},{5,6},{6,7},{8,9},{9,10},{10,11},{12,13},{... | collective-permute-start | bytes 27656 | tf_op jit(solution)/shard_map/ppermute | solution.py:32
  107.7 5.6 %collective-permute-start.11 = (f32[18,1,128]{2,1,0:T(1,128)S(1)}, f32[18,1,128]{2,1,0:T(1,128)S(1)}, u32[]{:S(2)}, u32[]{:S(2)}) collective-permute-start(f32[18,1,128]{2,1,0:T(1,128)S(1)} %get-tuple-element.27), channel_id=1, source_target_pairs={{1,0},{2,1},{3,2},{5,4},{6,5},{7,6},{9,8},{10,9},{11,10},{13,12},{... | collective-permute-start | bytes 27656 | tf_op jit(solution)/shard_map/ppermute | solution.py:35
  136.4 21.0 %copy-start.1 = (f32[3,7680]{1,0:T(4,128)S(1)}, f32[3,7680]{1,0:T(4,128)}, u32[]{:S(2)}) copy-start(f32[3,7680]{1,0:T(4,128)} %param.28) | copy-start | bytes 276484
  136.4 21.0 %copy-start.2 = (f32[3,7680]{1,0:T(4,128)S(1)}, f32[3,7680]{1,0:T(4,128)}, u32[]{:S(2)}) copy-start(f32[3,7680]{1,0:T(4,128)} %param.26) | copy-start | bytes 276484
  136.4 21.0 %copy-start.3 = (f32[3,7680]{1,0:T(4,128)S(1)}, f32[3,7680]{1,0:T(4,128)}, u32[]{:S(2)}) copy-start(f32[3,7680]{1,0:T(4,128)} %param.25) | copy-start | bytes 276484
  136.4 22.0 %copy-start.5 = (f32[8,128]{1,0:T(8,128)S(1)}, f32[8,128]{1,0:T(8,128)}, u32[]{:S(2)}) copy-start(f32[8,128]{1,0:T(8,128)} %get-tuple-element.12) | copy-start | bytes 12292
  157.3 160.6 %all-gather.2.cloned.1.call-start = ((), (), s32[]{:S(2)}) async-start(), calls=%async_computation | async-start | bytes 2457600 | tf_op jit(solution)/shard_map/all_gather | solution.py:370
  315.8 4.9 %copy-start.6 = (f32[3]{0:T(128)S(1)}, f32[3]{0:T(128)}, u32[]{:S(2)}) copy-start(f32[3]{0:T(128)} %constant.29.clone) | copy-start | bytes 40
  317.9 2.9 copy-start
Sparse Core Ops, SparseCore 0:
  157.4 157.1 all-reduce.5
Sparse Core Ops, SparseCore 1:
  159.3 46.5 all-gather.1

commit v2 on v1

--- a/solution.py
+++ b/solution.py
@@ -22,19 +22,6 @@
 F32, BF16 = jnp.float32, jnp.bfloat16
 VMEM = pltpu.VMEM
 SMEM = pltpu.SMEM
-
-
-def padded(block, sides, width):
-    for axis, dim in sides:
-        count = lax.axis_size(axis)
-        forward = [(i, i + 1) for i in range(count - 1)]
-        backward = [(target, source) for source, target in forward]
-        low = lax.ppermute(
-            lax.slice_in_dim(block, block.shape[dim] - width, None, axis=dim), axis, forward
-        )
-        high = lax.ppermute(lax.slice_in_dim(block, 0, width, axis=dim), axis, backward)
-        block = jnp.concatenate([low, block, high], axis=dim)
-    return block
 
 
 def pieces(x, count):
@@ -141,8 +128,6 @@
         fj_ref, p_out, error_ref, pb_ref, si_ref, ws_ref, wv_ref = rest
     rows, cols = p_ref.shape[0], p_ref.shape[1]
     if first:
-        for c0 in range(0, si_ref.shape[0], 1024):
-            pass
         build_near(pos_ref, base_ref, fj_ref, stage_ref, cols)
     si_ref[...] = jnp.zeros_like(si_ref)
     build_values(val_ref, pb_ref, cols)
@@ -177,7 +162,7 @@
     out_ref[...] = wv_ref[...] / (wall_offset + ws_ref[...]) * live_ref[...].astype(F32)
 
 
-def scatter_kernel(high, wp_ref, normal_ref, arm_ref, body_ref, out_ref, val_ref, lhs_ref, rhs_ref):
+def scatter_kernel(high, owned, shard, wp_ref, normal_ref, arm_ref, body_ref, out_ref, val_ref, lhs_ref, rhs_ref):
     rows, cols = wp_ref.shape[0], wp_ref.shape[1]
     out_ref[...] = jnp.zeros_like(out_ref)
     high_iota = lax.broadcasted_iota(jnp.int32, (high, 128), 0)
@@ -191,12 +176,10 @@
         for q, value in enumerate(values):
             for s, piece in enumerate(pieces(value, 2)):
                 val_ref[q * 2 + s] = piece
-        body = body_ref[r]
+        top, low = two_level(body_ref[r], owned, shard)
         for c in range(cols):
-            line = body[c : c + 1]
-            top = line // LOW
-            at_high = high_iota == top
-            at_low = (low_iota == line - top * LOW).astype(F32).astype(BF16)
+            at_high = high_iota == top[c : c + 1]
+            at_low = (low_iota == low[c : c + 1]).astype(F32).astype(BF16)
             for s in range(2):
                 lanes = slice((c * 2 + s) * 128, (c * 2 + s + 1) * 128)
                 rhs_ref[:, lanes] = at_low
@@ -213,7 +196,7 @@
     lax.fori_loop(0, rows, row, 0)
 
 
-def gather_kernel(high, state_ref, arm_ref, body_ref, out_ref, lhs_ref, got_ref):
+def gather_kernel(high, owned, shard, state_ref, arm_ref, body_ref, out_ref, lhs_ref, got_ref):
     rows, cols = body_ref.shape[0], body_ref.shape[1]
     for q in range(6):
         for s, piece in enumerate(pieces(state_ref[q], 2)):
@@ -222,12 +205,14 @@
     low_iota = lax.broadcasted_iota(jnp.int32, (LOW, 256), 0)
 
     def row(r, carry):
-        body = body_ref[r]
+        top, low = two_level(body_ref[r], owned, shard)
         for c in range(0, cols, 2):
-            line = jnp.concatenate([body[c : c + 1], body[c + 1 : c + 2]], axis=1)
-            top = line // LOW
-            at_high = (high_iota == top).astype(F32).astype(BF16)
-            at_low = low_iota == line - top * LOW
+            top_line, low_line = [
+                jnp.concatenate([line[c : c + 1], line[c + 1 : c + 2]], axis=1)
+                for line in (top, low)
+            ]
+            at_high = (high_iota == top_line).astype(F32).astype(BF16)
+            at_low = low_iota == low_line
             rhs = jnp.concatenate([at_high, at_high], axis=0)
             for q in range(6):
                 found = jnp.dot(
@@ -244,6 +229,307 @@
     out_ref[0] = vx + (wy * az - wz * ay)
     out_ref[1] = vy + (wz * ax - wx * az)
     out_ref[2] = vz + (wx * ay - wy * ax)
+
+
+def remote(src, dst, send, recv, device):
+    return pltpu.make_async_remote_copy(
+        src_ref=src,
+        dst_ref=dst,
+        send_sem=send,
+        recv_sem=recv,
+        device_id=device,
+        device_id_type=pl.DeviceIdType.MESH,
+    )
+
+
+WAYS = ((-1, 0), (1, 0), (0, -1), (0, 1), (-1, -1), (-1, 1), (1, -1), (1, 1))
+
+
+def halo_kernel(x_ref, out_ref, row_in, col_send, col_in, corner_send, corner_in, send, recv):
+    depth, rows, cols, _ = x_ref.shape
+    tiles, parts = lax.axis_size("tile"), lax.axis_size("body")
+    t, b = lax.axis_index("tile"), lax.axis_index("body")
+
+    def exists(dt, db):
+        ok = jnp.bool_(True)
+        if dt:
+            ok = (t > 0) if dt < 0 else (t < tiles - 1)
+        if db:
+            side = (b > 0) if db < 0 else (b < parts - 1)
+            ok = jnp.logical_and(ok, side) if dt else side
+        return ok
+
+    barrier = pltpu.get_barrier_semaphore()
+    for dt, db in WAYS:
+
+        @pl.when(exists(dt, db))
+        def _():
+            pl.semaphore_signal(
+                barrier, inc=1, device_id=(t + dt, b + db), device_id_type=pl.DeviceIdType.MESH
+            )
+
+    for side in range(2):
+        col_send[side] = x_ref[:, :, side * (cols - 1), :]
+    for n, (dt, db) in enumerate(WAYS[4:]):
+        r, c = (dt > 0) * (rows - 1), (db > 0) * (cols - 1)
+        for d in range(depth):
+            corner_send[n, d : d + 1] = x_ref[d, r, c : c + 1]
+
+    along = 1 + (t > 0).astype(jnp.int32) + (t < tiles - 1).astype(jnp.int32)
+    across = 1 + (b > 0).astype(jnp.int32) + (b < parts - 1).astype(jnp.int32)
+    pl.semaphore_wait(barrier, along * across - 1)
+
+    def copy(n):
+        dt, db = WAYS[n]
+        if n < 2:
+            src, dst = x_ref.at[:, (dt > 0) * (rows - 1)], row_in.at[n]
+        elif n < 4:
+            src, dst = col_send.at[n - 2], col_in.at[n - 2]
+        else:
+            src, dst = corner_send.at[n - 4], corner_in.at[n - 4]
+        return remote(src, dst, send.at[n], recv.at[n], (t + dt, b + db))
+
+    for n, (dt, db) in enumerate(WAYS):
+
+        @pl.when(exists(dt, db))
+        def _():
+            copy(n).start()
+
+    out_ref[...] = jnp.zeros_like(out_ref)
+    for d in range(depth):
+        for r in range(rows):
+            out_ref[d, r + 1, 1 : cols + 1] = x_ref[d, r]
+    for n, (dt, db) in enumerate(WAYS):
+
+        @pl.when(exists(-dt, -db))
+        def _():
+            copy(n).wait_recv()
+            r = 0 if dt > 0 else rows + 1
+            c = 0 if db > 0 else cols + 1
+            for d in range(depth):
+                if n < 2:
+                    out_ref[d, r, 1 : cols + 1] = row_in[n, d]
+                elif n < 4:
+                    for i in range(rows):
+                        out_ref[d, i + 1, c : c + 1] = col_in[n - 2, d, i : i + 1]
+                else:
+                    out_ref[d, r, c : c + 1] = corner_in[n - 4, d : d + 1]
+
+    for n, (dt, db) in enumerate(WAYS):
+
+        @pl.when(exists(dt, db))
+        def _():
+            copy(n).wait_send()
+
+
+def halo(x, number):
+    depth, rows, cols, _ = x.shape
+    wide = -(-(cols + 2) // 8) * 8
+    return pl.pallas_call(
+        halo_kernel,
+        out_shape=shape((depth, rows + 2, wide, 128)),
+        in_specs=[pl.BlockSpec(memory_space=VMEM)],
+        out_specs=pl.BlockSpec(memory_space=VMEM),
+        scratch_shapes=[
+            VMEM((2, depth, cols, 128), F32),
+            VMEM((2, depth, rows, 128), F32),
+            VMEM((2, depth, rows, 128), F32),
+            VMEM((4, 8, 128), F32),
+            VMEM((4, 8, 128), F32),
+            pltpu.SemaphoreType.DMA((8,)),
+            pltpu.SemaphoreType.DMA((8,)),
+        ],
+        compiler_params=pltpu.CompilerParams(collective_id=number, has_side_effects=True),
+        name="halo%d" % number,
+    )(x)
+
+
+def exchange_kernel(
+    per,
+    spare,
+    partial_ref,
+    error_ref,
+    params_ref,
+    full_ref,
+    own_ref,
+    error_out,
+    a_ref,
+    r1_ref,
+    s1_ref,
+    r2_ref,
+    s2_ref,
+    r3_ref,
+    g3_ref,
+    g2_ref,
+    g1_ref,
+    send1,
+    recv1,
+    send2,
+    recv2,
+    send3,
+    recv3,
+):
+    chips, parts = a_ref.shape[1], a_ref.shape[2]
+    shard = params_ref.shape[1] * per
+    high = parts * shard
+    t, b = lax.axis_index("tile"), lax.axis_index("body")
+    core, chip = t % 2, t // 2
+    barrier = pltpu.get_barrier_semaphore()
+    partner = (chip * 2 + 1 - core, b)
+    others2 = [(chip + k) % chips for k in range(1, chips)]
+    others3 = [(b + k) % parts for k in range(1, parts)]
+    greeted = [partner] + [(g * 2 + core, b) for g in others2] + [(t, g) for g in others3]
+    for device in greeted:
+        pl.semaphore_signal(barrier, inc=1, device_id=device, device_id_type=pl.DeviceIdType.MESH)
+
+    def place(q, k, g, p):
+        return q * high + p * shard + (g * 2 + k) * per
+
+    a_ref[...] = jnp.zeros_like(a_ref)
+    for k in range(2):
+        for g in range(chips):
+            for p in range(parts):
+                for q in range(6):
+                    at = place(q, k, g, p)
+                    a_ref[k, g, p, q * per : (q + 1) * per] = partial_ref[at : at + per]
+    owner, line = spare // per, spare % per
+    lane = lax.broadcasted_iota(jnp.int32, (1, LOW), 1)
+    a_ref[owner % 2, owner // 2, 0, line : line + 1] = jnp.where(
+        lane == 0, jnp.sum(error_ref[...]), 0.0
+    )
+    pl.semaphore_wait(barrier, len(greeted))
+
+    first = remote(a_ref.at[1 - core], r1_ref, send1.at[0], recv1.at[0], partner)
+    first.start()
+    first.wait()
+    s1_ref[...] = a_ref[core] + r1_ref[...]
+
+    copies = [
+        remote(s1_ref.at[g], r2_ref.at[chip], send2.at[g], recv2.at[chip], (g * 2 + core, b))
+        for g in others2
+    ]
+    for item in copies:
+        item.start()
+    total = s1_ref[chip]
+    for g in others2:
+        remote(s1_ref.at[g], r2_ref.at[g], send2.at[g], recv2.at[g], partner).wait_recv()
+        total = total + r2_ref[g]
+    s2_ref[...] = total
+    for item in copies:
+        item.wait_send()
+
+    copies = [
+        remote(s2_ref.at[g], r3_ref.at[b], send3.at[g], recv3.at[b], (t, g)) for g in others3
+    ]
+    for item in copies:
+        item.start()
+    total = s2_ref[b]
+    for g in others3:
+        remote(s2_ref.at[g], r3_ref.at[g], send3.at[g], recv3.at[g], partner).wait_recv()
+        total = total + r3_ref[g]
+    for item in copies:
+        item.wait_send()
+
+    g3_ref[b] = jnp.zeros_like(total)
+    mine = [params_ref[n, t] for n in range(10)]
+    for q in range(6):
+        moved = total[q * per : (q + 1) * per]
+        if q < 3:
+            state = mine[q] + time_step * (mine[6] * moved)
+        else:
+            state = mine[q] + time_step * mine[4 + q] * moved
+        if q == 2:
+            state = state + time_step * gravity_z
+        g3_ref[b, q * per : (q + 1) * per] = state
+
+    copies = [
+        remote(
+            g3_ref.at[b], g3_ref.at[b], send3.at[parts + g], recv3.at[parts + b], (t, g)
+        )
+        for g in others3
+    ]
+    for item in copies:
+        item.start()
+    for g in others3:
+        remote(
+            g3_ref.at[g], g3_ref.at[g], send3.at[parts + g], recv3.at[parts + g], partner
+        ).wait_recv()
+    for item in copies:
+        item.wait_send()
+
+    copies = [
+        remote(
+            g3_ref, g2_ref.at[chip], send2.at[chips + g], recv2.at[chips + chip], (g * 2 + core, b)
+        )
+        for g in others2
+    ]
+    for item in copies:
+        item.start()
+    g2_ref[chip] = g3_ref[...]
+    for g in others2:
+        remote(
+            g3_ref, g2_ref.at[g], send2.at[chips + g], recv2.at[chips + g], partner
+        ).wait_recv()
+    for item in copies:
+        item.wait_send()
+
+    last = remote(g2_ref, g1_ref.at[core], send1.at[1], recv1.at[1 + core], partner)
+    last.start()
+    g1_ref[core] = g2_ref[...]
+    remote(g2_ref, g1_ref.at[1 - core], send1.at[1], recv1.at[2 - core], partner).wait_recv()
+    last.wait_send()
+
+    for k in range(2):
+        for g in range(chips):
+            for q in range(6):
+                row = (g * 2 + k) * per
+                own_ref[q, row : row + per] = g1_ref[k, g, b, q * per : (q + 1) * per]
+                for p in range(parts):
+                    at = p * shard + row
+                    full_ref[q, at : at + per] = g1_ref[k, g, p, q * per : (q + 1) * per]
+    error_out[...] = g1_ref[owner % 2, owner // 2, 0, line : line + 1, 0:128]
+
+
+def exchange(partials, error, params, per, spare):
+    tiles, parts = lax.axis_size("tile"), lax.axis_size("body")
+    chips, shard = tiles // 2, params.shape[1] * per
+    lines = -(-6 * per // 8) * 8
+    chunk = (lines, LOW)
+    dma = pltpu.SemaphoreType.DMA
+    return pl.pallas_call(
+        functools.partial(exchange_kernel, per, spare),
+        out_shape=(shape((6, parts * shard, LOW)), shape((6, shard, LOW)), shape((1, 128))),
+        in_specs=[pl.BlockSpec(memory_space=VMEM)] * 3,
+        out_specs=(pl.BlockSpec(memory_space=VMEM),) * 3,
+        scratch_shapes=[
+            VMEM((2, chips, parts) + chunk, F32),
+            VMEM((chips, parts) + chunk, F32),
+            VMEM((chips, parts) + chunk, F32),
+            VMEM((chips, parts) + chunk, F32),
+            VMEM((parts,) + chunk, F32),
+            VMEM((parts,) + chunk, F32),
+            VMEM((parts,) + chunk, F32),
+            VMEM((chips, parts) + chunk, F32),
+            VMEM((2, chips, parts) + chunk, F32),
+            dma((2,)),
+            dma((3,)),
+            dma((2 * chips,)),
+            dma((2 * chips,)),
+            dma((2 * parts,)),
+            dma((2 * parts,)),
+        ],
+        compiler_params=pltpu.CompilerParams(
+            collective_id=9, has_side_effects=True, vmem_limit_bytes=40 * 2**20
+        ),
+        name="exchange",
+    )(partials, error, params)
+
+
+def two_level(body, owned, shard):
+    index = body
+    for part in range(1, lax.axis_size("body")):
+        index = index + jnp.where(body >= part * owned, shard * LOW - owned, 0)
+    return index // LOW, index % LOW
 
 
 def call(kernel, shapes, ins, scratch, spaces, name):
@@ -260,24 +546,6 @@
 
 def shape(dims, kind=F32):
     return jax.ShapeDtypeStruct(tuple(dims), kind)
-
-
-def wide_columns(block):
-    extra = -block.shape[-2] % 8
-    widths = [(0, 0)] * block.ndim
-    widths[-2] = (0, extra)
-    return jnp.pad(block, widths)
-
-
-def advance(params, totals):
-    lift = jnp.array([0.0, 0.0, time_step * gravity_z], dtype=F32)[:, None, None]
-    linear = params[0:3] + time_step * (params[6][None] * totals[0:3]) + lift
-    angular = params[3:6] + time_step * params[7:10] * totals[3:6]
-    return jnp.concatenate([linear, angular], 0)
-
-
-def widened(values):
-    return wide_columns(padded(values, (("tile", 0), ("body", 1)), 1))
 
 
 def shards(
@@ -299,13 +567,7 @@
     rows, cols, _ = fluid_pressure.shape
     blocks = (rows + 2) * (cols + 2)
     base = jnp.stack([lax.axis_index("tile") * rows, lax.axis_index("body") * cols]).astype(jnp.int32)
-    both = wide_columns(
-        padded(
-            jnp.concatenate([fluid_position, fluid_pressure[None]], 0),
-            (("tile", 1), ("body", 2)),
-            1,
-        )
-    )
+    both = halo(jnp.concatenate([fluid_position, fluid_pressure[None]], 0), 1)
     padded_pos, padded_val = both[:3], both[3]
     wide = padded_pos.shape[2]
     small = shape((rows, cols, 128))
@@ -331,7 +593,7 @@
     pressure, error = call(
         second,
         (small, shape((cols, 128))),
-        (base, neighbours, fluid_position, widened(pressure), pressure, source, stiffness, near),
+        (base, neighbours, fluid_position, halo(pressure[None], 2)[0], pressure, source, stiffness, near),
         pair_scratch,
         [SMEM] * 2 + [VMEM] * 6,
         "sweep_second",
@@ -339,21 +601,20 @@
     wall_pressure = call(
         wall_kernel,
         small,
-        (base, neighbours, wall_position, widened(pressure), wall_live, near),
+        (base, neighbours, wall_position, halo(pressure[None], 3)[0], wall_live, near),
         pair_scratch,
         [SMEM] * 2 + [VMEM] * 4,
         "wall",
     )
     particle_total = rows * cols * 128 * lax.axis_size("tile") * lax.axis_size("body")
-    error_local = jnp.sum(error) / particle_total
-
-    bodies_own = inverse_mass.shape[0]
-    bodies = bodies_own * lax.axis_size("body")
-    count = -(-bodies // LOW)
-    high = -(-count // 16) * 16
-    high = max(high, 128)
+    owned = inverse_mass.shape[0]
+    tiles = lax.axis_size("tile")
+    spare = -(-owned // LOW)
+    per = spare // tiles + 1
+    shard = per * tiles
+    high = shard * lax.axis_size("body")
     partials = call(
-        functools.partial(scatter_kernel, high),
+        functools.partial(scatter_kernel, high, owned, shard),
         shape((6 * high, LOW)),
         (wall_pressure, wall_normal, wall_arm, wall_body),
         [
@@ -364,17 +625,16 @@
         [VMEM] * 4,
         "scatter",
     )
-    own_params = jnp.concatenate(
+    params = jnp.concatenate(
         [linear_velocity, angular_velocity, inverse_mass[None], inverse_inertia], 0
     )
-    all_params = lax.all_gather(own_params, "body", axis=1, tiled=True)
-    all_params = jnp.pad(all_params, ((0, 0), (0, high * LOW - bodies))).reshape(10, high, LOW)
-    totals, density_error = lax.psum((partials, error_local), ("tile", "body"))
-    full_state = advance(all_params, totals.reshape(6, high, LOW))
-    flat = full_state.reshape(6, high * LOW)
-    own_state = lax.dynamic_slice_in_dim(flat, lax.axis_index("body") * bodies_own, bodies_own, 1)
+    fill = jnp.zeros((10, shard * LOW - owned), F32).at[6].set(1.0 / time_step)
+    params = jnp.concatenate([params, fill], 1).reshape(10, tiles, per, LOW)
+    full_state, own_state, error = exchange(partials, error, params, per, spare)
+    own_state = own_state.reshape(6, shard * LOW)[:, :owned]
+    density_error = error[0, 0] / particle_total
     wall_velocity = call(
-        functools.partial(gather_kernel, high),
+        functools.partial(gather_kernel, high, owned, shard),
         shape((3, rows, cols, 128)),
         (full_state, wall_arm, wall_body),
         [VMEM((6 * LOW, 2 * high), BF16), VMEM((6, rows, cols, 128), F32)],

time: 352 us -> 174 us (0.49)
  waiting for transfers between devices: 131 us -> 0 us
  Pallas kernels: 112 us -> 161 us
  blocking collectives: 42.9 us -> 0 us
  starting transfers between devices: 26.4 us -> 0 us
  between operations: 16.4 us -> 1.96 us
  other arithmetic: 10.4 us -> 2.54 us
  local copies, waits for them, and re-layouts: 12.2 us -> 7.98 us
    psum x1 -> x0, waiting for transfers between devices: 112 us -> none  [shards(): totals, density_error = lax.psum((partials, error_local), ('tile', 'body'))]
    pallas_call x0 -> x4, Pallas kernels: none -> 49 us  [the longest x1 27.6 us: exchange(): pl.pallas_call(functools.partial(exchange_kernel, per, spare), out_shape=...]
    psum x1 -> x0, blocking collectives: 42.9 us -> none  [shards(): totals, density_error = lax.psum((partials, error_local), ('tile', 'body'))]
    ppermute x12 -> x0, starting transfers between devices: 26.3 us -> none  [the longest x6 18.6 us: padded(): lax.ppermute(lax.slice_in_dim(block, block.shape[dim] - width, None, axis...]
    ppermute x12 -> x0, waiting for transfers between devices: 18.6 us -> none  [the longest x6 18.5 us: padded(): lax.ppermute(lax.slice_in_dim(block, 0, width, axis=dim), axis, backward)]
    slice x9 -> x1, local copies, waits for them, and re-layouts: 7.49 us -> 0.71 us  [shards(): own_state = own_state.reshape(6, shard * LOW)[:, :owned]]
    slice x3 -> x0, other arithmetic: 3.65 us -> none  [the longest x2 1.91 us: padded(): lax.slice_in_dim(block, block.shape[dim] - width, None, axis=dim)]
  transfers between devices with their start and end apart: 14 -> 0, of which waited for: 8 -> 0; matrix products, arithmetic and copies ran while one was open for 2% -> 0% of each run, Pallas kernels for 0% -> 0%
where the time goes in v2:
time: 174 us; the launch traced here: 173 us
  Pallas kernels  161 us (93%)
  local copies, waits for them, and re-layouts  7.98 us (5%)
  other arithmetic  2.54 us (1%)
  between operations  1.96 us (1%)
    pallas_call x5, Pallas kernels, call(): pl.pallas_call(kernel, out_shape=shapes, in_specs=[pl.BlockSpec(memory_sp...  112 us
    pallas_call x1, Pallas kernels, exchange(): pl.pallas_call(functools.partial(exchange_kernel, per, spare), out_shape=...  27.6 us
    pallas_call x3, Pallas kernels, halo(): pl.pallas_call(halo_kernel, out_shape=shape((depth, rows + 2, wide, 128))...  21.4 us
    unnamed x18, local copies, waits for them, and re-layouts  3.64 us

profile of v2, /device:TPU:0, one launch (start us, length us, event | category | flops | bytes accessed | tf_op | source)
XLA Modules:
  0.0 173.1 jit_solution(9020928770056610690)
XLA Ops:
  0.6 0.7 pad_add_fusion.base_ref
  1.3 1.5 copy.20.near_ref
  2.8 1.7 pad_maximum_fusion.1.x_ref
  4.5 8.9 %halo1.1 = f32[4,18,16,128]{3,2,1,0:T(8,128)} custom-call(f32[4,16,8,128]{3,2,1,0:T(8,128)} %pad_maximum_fusion.1.x_ref), custom_call_target="tpu_custom_call" | custom-call | tf_op jit(solution)/shard_map/halo1/pallas_call | solution.py:328
  13.4 1.8 %slice.26.pos_ref = f32[3,18,16,128]{3,2,1,0:T(8,128)} slice(f32[4,18,16,128]{3,2,1,0:T(8,128)} %halo1.1), slice={[0:3], [0:18], [0:16], [0:128]} | slice | bytes 884736 | tf_op jit(solution)/shard_map/slice | solution.py:571
  15.2 1.6 slice_bitcast_fusion.val_ref
  16.8 27.1 %sweep_first.1 = (f32[16,8,128]{2,1,0:T(8,128)}, bf16[23040,128]{1,0:T(8,128)(2,1)}) custom-call(s32[2]{0:T(128)} %pad_add_fusion.base_ref, s32[16,8,6]{2,1,0:T(8,128)} %copy.20.near_ref, f32[3,18,16,128]{3,2,1,0:T(8,128)} %slice.26.pos_ref, f32[3,16,8,128]{3,2,1,0:T(8,128)} %own_ref.4, f32[18,16,128]{2,1,0:T(8,128)} %slice_bitcast_fusion.val_ref, ...), custom_call_target="tpu_custom_call" | custom-call | tf_op jit(solution)/shard_map/sweep_first/pallas_call | solution.py:536
  43.8 5.9 %halo2.1 = f32[1,18,16,128]{3,2,1,0:T(8,128)} custom-call(f32[1,16,8,128]{3,2,1,0:T(8,128)} %bitcast.18), custom_call_target="tpu_custom_call" | custom-call | tf_op jit(solution)/shard_map/halo2/pallas_call | solution.py:328
  49.7 0.0 copy-start.6
  49.8 0.0 copy-start.3
  49.8 0.0 copy-start.4
  49.8 0.0 copy-start.5
  49.8 0.0 copy-start.7
  49.8 22.5 %sweep_second.1 = (f32[16,8,128]{2,1,0:T(8,128)}, f32[8,128]{1,0:T(8,128)}) custom-call(s32[2]{0:T(128)} %pad_add_fusion.base_ref, s32[16,8,6]{2,1,0:T(8,128)} %copy.20.near_ref, f32[3,16,8,128]{3,2,1,0:T(8,128)} %own_ref.4, f32[18,16,128]{2,1,0:T(8,128)} %bitcast.16, f32[16,8,128]{2,1,0:T(8,128)} %get-tuple-element.24.rest_0_, f32[16,8,128]{2,1,0:T(8,128)} %rest_1_.1, ...), custom_call_target="tpu_custom_call" | custom-call | tf_op jit(solution)/shard_map/sweep_second/pallas_call | solution.py:536
  72.3 6.7 %halo3.1 = f32[1,18,16,128]{3,2,1,0:T(8,128)} custom-call(f32[1,16,8,128]{3,2,1,0:T(8,128)} %bitcast.20), custom_call_target="tpu_custom_call" | custom-call | tf_op jit(solution)/shard_map/halo3/pallas_call | solution.py:328
  79.0 22.4 %wall.1.wp_ref = f32[16,8,128]{2,1,0:T(8,128)} custom-call(s32[2]{0:T(128)} %pad_add_fusion.base_ref, s32[16,8,6]{2,1,0:T(8,128)} %copy.20.near_ref, f32[3,16,8,128]{3,2,1,0:T(8,128)} %own_ref.5, f32[18,16,128]{2,1,0:T(8,128)} %bitcast.17, s32[16,8,128]{2,1,0:T(8,128)} %live_ref.1, bf16[23040,128]{1,0:T(8,128)(2,1)} %get-tuple-element.25.rest_3_.fj_ref), custom_call_target="tpu_custom_call" | custom-call | tf_op jit(solution)/shard_map/wall/pallas_call | solution.py:536
  101.4 20.9 %scatter.1.partial_ref = f32[768,256]{1,0:T(8,128)} custom-call(f32[16,8,128]{2,1,0:T(8,128)} %wall.1.wp_ref, f32[3,16,8,128]{3,2,1,0:T(8,128)} %normal_ref.1, f32[3,16,8,128]{3,2,1,0:T(8,128)} %arm_ref.3, s32[16,8,128]{2,1,0:T(8,128)} %body_ref.3), custom_call_target="tpu_custom_call" | custom-call | tf_op jit(solution)/shard_map/scatter/pallas_call | solution.py:536
  122.2 0.0 copy-done.6
  122.3 0.0 copy-done.3
  122.3 0.0 copy-done.4
  122.3 0.0 copy-done.5
  122.3 0.0 copy-done.7
  122.3 0.2 pad_maximum_fusion
  122.5 0.2 reshape.40.params_ref
  122.7 0.0 copy-done.2
  122.7 0.0 copy-start
  122.7 1.1 copy-done
  123.9 27.6 %exchange.1 = (f32[6,128,256]{2,1,0:T(8,128)S(1)}, f32[6,32,256]{2,1,0:T(8,128)S(1)}, f32[1,128]{1,0:T(1,128)S(1)}) custom-call(f32[768,256]{1,0:T(8,128)S(1)} %copy-done, f32[8,128]{1,0:T(8,128)S(1)} %copy-done.2, f32[10,8,4,256]{3,2,1,0:T(4,128)S(1)} %reshape.40.params_ref), custom_call_target="tpu_custom_call" | custom-call | tf_op jit(solution)/shard_map/exchange/pallas_call | solution.py:499
  151.4 0.9 copy-done.1
  152.3 0.1 copy.22
  152.4 0.7 slice.30
  153.1 18.8 %gather.1 = f32[3,16,8,128]{3,2,1,0:T(8,128)} custom-call(f32[6,128,256]{2,1,0:T(8,128)} %copy-done.1, f32[3,16,8,128]{3,2,1,0:T(8,128)} %arm_ref.3, s32[16,8,128]{2,1,0:T(8,128)} %body_ref.3), custom_call_target="tpu_custom_call" | custom-call | tf_op jit(solution)/shard_map/gather/pallas_call | solution.py:536
  (3 shorter events, 0.0 us)
Async XLA Ops:
  49.7 72.5 %copy-start.6 = (f32[7680]{0:T(1024)S(1)}, f32[7680]{0:T(1024)}, u32[]{:S(2)}) copy-start(f32[7680]{0:T(1024)} %param.28) | copy-start | bytes 92164
  49.8 72.5 %copy-start.3 = (f32[3,7680]{1,0:T(4,128)S(1)}, f32[3,7680]{1,0:T(4,128)}, u32[]{:S(2)}) copy-start(f32[3,7680]{1,0:T(4,128)} %param.29) | copy-start | bytes 276484
  49.8 72.5 %copy-start.4 = (f32[3,7680]{1,0:T(4,128)S(1)}, f32[3,7680]{1,0:T(4,128)}, u32[]{:S(2)}) copy-start(f32[3,7680]{1,0:T(4,128)} %param.27) | copy-start | bytes 276484
  49.8 72.5 %copy-start.5 = (f32[3,7680]{1,0:T(4,128)S(1)}, f32[3,7680]{1,0:T(4,128)}, u32[]{:S(2)}) copy-start(f32[3,7680]{1,0:T(4,128)} %param.26) | copy-start | bytes 276484
  49.8 72.5 %copy-start.7 = (f32[10,512]{1,0:T(8,128)S(1)}, f32[10,512]{1,0:T(8,128)}, u32[]{:S(2)}) copy-start(f32[10,512]{1,0:T(8,128)} %constant.46.clone.1) | copy-start | bytes 61444
  72.3 50.4 %copy-start.2 = (f32[8,128]{1,0:T(8,128)S(1)}, f32[8,128]{1,0:T(8,128)}, u32[]{:S(2)}) copy-start(f32[8,128]{1,0:T(8,128)} %get-tuple-element.27.error_ref) | copy-start | bytes 12292
  122.7 1.1 copy-start
  151.4 0.9 copy-start.1

commit v3 on v2

--- a/solution.py
+++ b/solution.py
@@ -102,7 +102,7 @@
         wv = jnp.zeros((8, 128), F32)
         for k in range(listed):
             code = near_ref[r, c, k]
-            up = code // 3
+            up = (code * 11) >> 5
             block = (r + up) * (cols + 2) + c + code - up * 3
             start = pl.multiple_of(block * 128, 128)
             features = si_ref[pl.ds(code * (DEPTH * cols) + c, DEPTH, stride=cols), :]
@@ -529,7 +529,7 @@
     index = body
     for part in range(1, lax.axis_size("body")):
         index = index + jnp.where(body >= part * owned, shard * LOW - owned, 0)
-    return index // LOW, index % LOW
+    return index >> (LOW.bit_length() - 1), index & (LOW - 1)
 
 
 def call(kernel, shapes, ins, scratch, spaces, name):
@@ -568,8 +568,7 @@
     blocks = (rows + 2) * (cols + 2)
     base = jnp.stack([lax.axis_index("tile") * rows, lax.axis_index("body") * cols]).astype(jnp.int32)
     both = halo(jnp.concatenate([fluid_position, fluid_pressure[None]], 0), 1)
-    padded_pos, padded_val = both[:3], both[3]
-    wide = padded_pos.shape[2]
+    wide = both.shape[2]
     small = shape((rows, cols, 128))
     fj_shape = (blocks * 128, 128)
     pair_scratch = [
@@ -578,12 +577,17 @@
         VMEM((rows, cols, 128), F32),
         VMEM((rows, cols, 128), F32),
     ]
+    def opening(base_ref, near_ref, both_ref, own_ref, *rest):
+        sweep_kernel(
+            True, base_ref, near_ref, both_ref, own_ref, both_ref.at[both_ref.shape[0] - 1], *rest
+        )
+
     pressure, near = call(
-        functools.partial(sweep_kernel, True),
+        opening,
         (small, shape(fj_shape, BF16)),
-        (base, neighbours, padded_pos, fluid_position, padded_val, fluid_pressure, source, stiffness),
+        (base, neighbours, both, fluid_position, fluid_pressure, source, stiffness),
         pair_scratch + [VMEM((DEPTH * wide, 128), F32)],
-        [SMEM] * 2 + [VMEM] * 6,
+        [SMEM] * 2 + [VMEM] * 5,
         "sweep_first",
     )
 

time: 174 us -> 169 us (0.971)
  local copies, waits for them, and re-layouts: 7.98 us -> 4.58 us
    slice x1 -> x0, local copies, waits for them, and re-layouts: 1.81 us -> none  [shards(): padded_pos, padded_val = (both[:3], both[3])]
where the time goes in v3:
time: 169 us
  Pallas kernels  160 us (95%)
  local copies, waits for them, and re-layouts  4.58 us (3%)
  other arithmetic  2.53 us (1%)
  between operations  1.96 us (1%)
    pallas_call x5, Pallas kernels, call(): pl.pallas_call(kernel, out_shape=shapes, in_specs=[pl.BlockSpec(memory_sp...  111 us
    pallas_call x1, Pallas kernels, exchange(): pl.pallas_call(functools.partial(exchange_kernel, per, spare), out_shape=...  27.6 us
    pallas_call x3, Pallas kernels, halo(): pl.pallas_call(halo_kernel, out_shape=shape((depth, rows + 2, wide, 128))...  21.4 us
    unnamed x18, local copies, waits for them, and re-layouts  3.64 us

profile of v3, /device:TPU:0, one launch (start us, length us, event | category | flops | bytes accessed | tf_op | source)
XLA Modules:
  0.0 168.9 jit_solution(9732074850039945726)
XLA Ops:
  0.6 0.7 pad_add_fusion.base_ref
  1.3 1.5 copy.20.near_ref
  2.8 1.7 %pad_maximum_fusion.1.x_ref = f32[4,16,8,128]{3,2,1,0:T(8,128)} fusion(f32[1,16,8,128]{3,2,1,0:T(8,128)} %bitcast.17, f32[3,16,8,128]{3,2,1,0:T(8,128)} %own_ref.4), kind=kLoop, calls=%fused_computation.1 | loop fusion | flops 65536 | bytes 524288 | tf_op jit(solution)/shard_map/concatenate | solution.py:570
  4.5 8.9 %halo1.1.both_ref = f32[4,18,16,128]{3,2,1,0:T(8,128)} custom-call(f32[4,16,8,128]{3,2,1,0:T(8,128)} %pad_maximum_fusion.1.x_ref), custom_call_target="tpu_custom_call" | custom-call | tf_op jit(solution)/shard_map/halo1/pallas_call | solution.py:328
  13.4 26.9 %sweep_first.1 = (f32[16,8,128]{2,1,0:T(8,128)}, bf16[23040,128]{1,0:T(8,128)(2,1)}) custom-call(s32[2]{0:T(128)} %pad_add_fusion.base_ref, s32[16,8,6]{2,1,0:T(8,128)} %copy.20.near_ref, f32[4,18,16,128]{3,2,1,0:T(8,128)} %halo1.1.both_ref, f32[3,16,8,128]{3,2,1,0:T(8,128)} %own_ref.4, f32[16,8,128]{2,1,0:T(8,128)} %rest_0_.1, f32[16,8,128]{2,1,0:T(8,128)} %rest_1_.3, ...), custom_call_target="tpu_custom_call" | custom-call | tf_op jit(solution)/shard_map/sweep_first/pallas_call | solution.py:536
  40.3 5.9 %halo2.1 = f32[1,18,16,128]{3,2,1,0:T(8,128)} custom-call(f32[1,16,8,128]{3,2,1,0:T(8,128)} %bitcast.16), custom_call_target="tpu_custom_call" | custom-call | tf_op jit(solution)/shard_map/halo2/pallas_call | solution.py:328
  46.2 0.0 copy-start.6
  46.2 0.0 copy-start.3
  46.2 0.0 copy-start.4
  46.2 0.0 copy-start.5
  46.2 0.0 copy-start.7
  46.2 22.3 %sweep_second.1 = (f32[16,8,128]{2,1,0:T(8,128)}, f32[8,128]{1,0:T(8,128)}) custom-call(s32[2]{0:T(128)} %pad_add_fusion.base_ref, s32[16,8,6]{2,1,0:T(8,128)} %copy.20.near_ref, f32[3,16,8,128]{3,2,1,0:T(8,128)} %own_ref.4, f32[18,16,128]{2,1,0:T(8,128)} %bitcast.14, f32[16,8,128]{2,1,0:T(8,128)} %get-tuple-element.24.rest_0_, f32[16,8,128]{2,1,0:T(8,128)} %rest_1_.3, ...), custom_call_target="tpu_custom_call" | custom-call | tf_op jit(solution)/shard_map/sweep_second/pallas_call | solution.py:536
  68.5 0.0 copy-start.2
  68.5 6.7 %halo3.1 = f32[1,18,16,128]{3,2,1,0:T(8,128)} custom-call(f32[1,16,8,128]{3,2,1,0:T(8,128)} %bitcast.18), custom_call_target="tpu_custom_call" | custom-call | tf_op jit(solution)/shard_map/halo3/pallas_call | solution.py:328
  75.2 22.1 %wall.1.wp_ref = f32[16,8,128]{2,1,0:T(8,128)} custom-call(s32[2]{0:T(128)} %pad_add_fusion.base_ref, s32[16,8,6]{2,1,0:T(8,128)} %copy.20.near_ref, f32[3,16,8,128]{3,2,1,0:T(8,128)} %own_ref.5, f32[18,16,128]{2,1,0:T(8,128)} %bitcast.15, s32[16,8,128]{2,1,0:T(8,128)} %live_ref.1, bf16[23040,128]{1,0:T(8,128)(2,1)} %get-tuple-element.25.rest_3_.fj_ref), custom_call_target="tpu_custom_call" | custom-call | tf_op jit(solution)/shard_map/wall/pallas_call | solution.py:536
  97.3 20.8 %scatter.1.partial_ref = f32[768,256]{1,0:T(8,128)} custom-call(f32[16,8,128]{2,1,0:T(8,128)} %wall.1.wp_ref, f32[3,16,8,128]{3,2,1,0:T(8,128)} %normal_ref.1, f32[3,16,8,128]{3,2,1,0:T(8,128)} %arm_ref.3, s32[16,8,128]{2,1,0:T(8,128)} %body_ref.3), custom_call_target="tpu_custom_call" | custom-call | tf_op jit(solution)/shard_map/scatter/pallas_call | solution.py:536
  118.1 0.0 copy-done.6
  118.1 0.0 copy-done.3
  118.1 0.0 copy-done.4
  118.2 0.0 copy-done.5
  118.2 0.0 copy-done.7
  118.2 0.2 pad_maximum_fusion
  118.4 0.2 reshape.40.params_ref
  118.6 0.0 copy-done.2
  118.6 0.0 copy-start
  118.6 1.1 copy-done
  119.7 27.6 %exchange.1 = (f32[6,128,256]{2,1,0:T(8,128)S(1)}, f32[6,32,256]{2,1,0:T(8,128)S(1)}, f32[1,128]{1,0:T(1,128)S(1)}) custom-call(f32[768,256]{1,0:T(8,128)S(1)} %copy-done, f32[8,128]{1,0:T(8,128)S(1)} %copy-done.2, f32[10,8,4,256]{3,2,1,0:T(4,128)S(1)} %reshape.40.params_ref), custom_call_target="tpu_custom_call" | custom-call | tf_op jit(solution)/shard_map/exchange/pallas_call | solution.py:499
  147.3 0.0 copy-start.1
  147.3 0.9 copy-done.1
  148.2 0.1 copy.22
  148.3 0.7 slice.22
  149.0 18.7 %gather.1 = f32[3,16,8,128]{3,2,1,0:T(8,128)} custom-call(f32[6,128,256]{2,1,0:T(8,128)} %copy-done.1, f32[3,16,8,128]{3,2,1,0:T(8,128)} %arm_ref.3, s32[16,8,128]{2,1,0:T(8,128)} %body_ref.3), custom_call_target="tpu_custom_call" | custom-call | tf_op jit(solution)/shard_map/gather/pallas_call | solution.py:536
  (1 shorter events, 0.0 us)
Async XLA Ops:
  46.2 71.9 %copy-start.6 = (f32[7680]{0:T(1024)S(1)}, f32[7680]{0:T(1024)}, u32[]{:S(2)}) copy-start(f32[7680]{0:T(1024)} %param.28) | copy-start | bytes 92164
  46.2 72.0 %copy-start.3 = (f32[3,7680]{1,0:T(4,128)S(1)}, f32[3,7680]{1,0:T(4,128)}, u32[]{:S(2)}) copy-start(f32[3,7680]{1,0:T(4,128)} %param.29) | copy-start | bytes 276484
  46.2 72.0 %copy-start.4 = (f32[3,7680]{1,0:T(4,128)S(1)}, f32[3,7680]{1,0:T(4,128)}, u32[]{:S(2)}) copy-start(f32[3,7680]{1,0:T(4,128)} %param.27) | copy-start | bytes 276484
  46.2 72.0 %copy-start.5 = (f32[3,7680]{1,0:T(4,128)S(1)}, f32[3,7680]{1,0:T(4,128)}, u32[]{:S(2)}) copy-start(f32[3,7680]{1,0:T(4,128)} %param.26) | copy-start | bytes 276484
  46.2 72.0 %copy-start.7 = (f32[10,512]{1,0:T(8,128)S(1)}, f32[10,512]{1,0:T(8,128)}, u32[]{:S(2)}) copy-start(f32[10,512]{1,0:T(8,128)} %constant.46.clone.1) | copy-start | bytes 61444
  68.5 50.1 %copy-start.2 = (f32[8,128]{1,0:T(8,128)S(1)}, f32[8,128]{1,0:T(8,128)}, u32[]{:S(2)}) copy-start(f32[8,128]{1,0:T(8,128)} %get-tuple-element.27.error_ref) | copy-start | bytes 12292
  118.6 1.1 copy-start
  147.3 0.9 copy-start.1

commit v4 on v3

--- a/solution.py
+++ b/solution.py
@@ -70,7 +70,8 @@
         for c in range(cols + 2):
             features = stage_ref[pl.ds(c, DEPTH, stride=wide), :]
             start = pl.multiple_of((r * (cols + 2) + c) * 128, 128)
-            fj_ref[pl.ds(start, 128), 0:DEPTH] = features.T.astype(BF16)
+            twice = jnp.concatenate([features, features], axis=0)
+            fj_ref[pl.ds(start, 128), 0 : 2 * DEPTH] = twice.T.astype(BF16)
         return carry
 
     lax.fori_loop(0, rows, row, 0)
@@ -97,24 +98,36 @@
             at = (q * DEPTH + k) * cols
             si_ref[at : at + cols] = value
     listed = near_ref.shape[2]
+    lane = lax.broadcasted_iota(jnp.int32, (128, 2 * DEPTH), 1)
+    early = (lane < DEPTH).astype(F32).astype(BF16)
+    late = (lane >= DEPTH).astype(F32).astype(BF16)
+    blank = jnp.zeros((DEPTH, 128), BF16)
     for c in range(cols):
         ws = jnp.zeros((8, 128), F32)
         wv = jnp.zeros((8, 128), F32)
-        for k in range(listed):
-            code = near_ref[r, c, k]
-            up = (code * 11) >> 5
-            block = (r + up) * (cols + 2) + c + code - up * 3
-            start = pl.multiple_of(block * 128, 128)
-            features = si_ref[pl.ds(code * (DEPTH * cols) + c, DEPTH, stride=cols), :]
-            exponent = jnp.dot(
-                fj_ref[pl.ds(start, 128), 0:DEPTH],
-                features.astype(BF16),
-                preferred_element_type=F32,
+        for k in range(0, listed, 2):
+            starts, sides = [], []
+            for code in (near_ref[r, c, k], near_ref[r, c, k + 1]):
+                up = (code * 11) >> 5
+                block = (r + up) * (cols + 2) + c + code - up * 3
+                starts.append(pl.multiple_of(block * 128, 128))
+                at = code * (DEPTH * cols) + c
+                sides.append(si_ref[pl.ds(at, DEPTH, stride=cols), :].astype(BF16))
+            left = fj_ref[pl.ds(starts[0], 128), 0 : 2 * DEPTH] * early
+            left = left + fj_ref[pl.ds(starts[1], 128), 0 : 2 * DEPTH] * late
+            right = jnp.concatenate(
+                [
+                    jnp.concatenate([sides[0], blank], axis=1),
+                    jnp.concatenate([blank, sides[1]], axis=1),
+                ],
+                axis=0,
             )
-            weight = jnp.exp2(exponent)
-            product = weight * pb_ref[pl.ds(start, 128), :]
-            ws = ws + jnp.sum(weight.reshape(16, 8, 128), axis=0)
-            wv = wv + jnp.sum(product.reshape(16, 8, 128), axis=0)
+            weights = jnp.exp2(jnp.dot(left, right, preferred_element_type=F32))
+            for half, start in enumerate(starts):
+                weight = weights[:, half * 128 : (half + 1) * 128]
+                product = weight * pb_ref[pl.ds(start, 128), :]
+                ws = ws + jnp.sum(weight.reshape(16, 8, 128), axis=0)
+                wv = wv + jnp.sum(product.reshape(16, 8, 128), axis=0)
         ws_ref[r, c : c + 1] = jnp.sum(ws, axis=0, keepdims=True) * kernel_scale
         wv_ref[r, c : c + 1] = jnp.sum(wv, axis=0, keepdims=True) * kernel_scale
 

time: 169 us -> 174 us (1.030)
  Pallas kernels: 160 us -> 165 us
    pallas_call x5, Pallas kernels: 111 us -> 116 us  [call(): pl.pallas_call(kernel, out_shape=shapes, in_specs=[pl.BlockSpec(memory_sp...]
where the time goes in v4:
time: 174 us
  Pallas kernels  165 us (95%)
  local copies, waits for them, and re-layouts  4.58 us (3%)
  other arithmetic  2.53 us (1%)
  between operations  1.96 us (1%)
    pallas_call x5, Pallas kernels, call(): pl.pallas_call(kernel, out_shape=shapes, in_specs=[pl.BlockSpec(memory_sp...  116 us
    pallas_call x1, Pallas kernels, exchange(): pl.pallas_call(functools.partial(exchange_kernel, per, spare), out_shape=...  27.6 us
    pallas_call x3, Pallas kernels, halo(): pl.pallas_call(halo_kernel, out_shape=shape((depth, rows + 2, wide, 128))...  21.4 us
    unnamed x18, local copies, waits for them, and re-layouts  3.64 us

profile of v4, /device:TPU:0, one launch (start us, length us, event | category | flops | bytes accessed | tf_op | source)
XLA Modules:
  0.0 173.7 jit_solution(10262203826464421876)
XLA Ops:
  0.6 0.7 pad_add_fusion.base_ref
  1.3 1.5 copy.20.near_ref
  2.8 1.7 pad_maximum_fusion.1.x_ref
  4.5 8.9 %halo1.1.both_ref = f32[4,18,16,128]{3,2,1,0:T(8,128)} custom-call(f32[4,16,8,128]{3,2,1,0:T(8,128)} %pad_maximum_fusion.1.x_ref), custom_call_target="tpu_custom_call" | custom-call | tf_op jit(solution)/shard_map/halo1/pallas_call | solution.py:341
  13.4 28.5 %sweep_first.1 = (f32[16,8,128]{2,1,0:T(8,128)}, bf16[23040,128]{1,0:T(8,128)(2,1)}) custom-call(s32[2]{0:T(128)} %pad_add_fusion.base_ref, s32[16,8,6]{2,1,0:T(8,128)} %copy.20.near_ref, f32[4,18,16,128]{3,2,1,0:T(8,128)} %halo1.1.both_ref, f32[3,16,8,128]{3,2,1,0:T(8,128)} %own_ref.4, f32[16,8,128]{2,1,0:T(8,128)} %rest_0_.1, f32[16,8,128]{2,1,0:T(8,128)} %rest_1_.3, ...), custom_call_target="tpu_custom_call" | custom-call | tf_op jit(solution)/shard_map/sweep_first/pallas_call | solution.py:549
  41.9 5.9 %halo2.1 = f32[1,18,16,128]{3,2,1,0:T(8,128)} custom-call(f32[1,16,8,128]{3,2,1,0:T(8,128)} %bitcast.16), custom_call_target="tpu_custom_call" | custom-call | tf_op jit(solution)/shard_map/halo2/pallas_call | solution.py:341
  47.8 0.0 copy-start.6
  47.8 0.0 copy-start.3
  47.8 0.0 copy-start.4
  47.8 0.0 copy-start.5
  47.8 0.0 copy-start.7
  47.8 23.9 %sweep_second.1 = (f32[16,8,128]{2,1,0:T(8,128)}, f32[8,128]{1,0:T(8,128)}) custom-call(s32[2]{0:T(128)} %pad_add_fusion.base_ref, s32[16,8,6]{2,1,0:T(8,128)} %copy.20.near_ref, f32[3,16,8,128]{3,2,1,0:T(8,128)} %own_ref.4, f32[18,16,128]{2,1,0:T(8,128)} %bitcast.14, f32[16,8,128]{2,1,0:T(8,128)} %get-tuple-element.24.rest_0_, f32[16,8,128]{2,1,0:T(8,128)} %rest_1_.3, ...), custom_call_target="tpu_custom_call" | custom-call | tf_op jit(solution)/shard_map/sweep_second/pallas_call | solution.py:549
  71.8 0.0 copy-start.2
  71.8 6.7 %halo3.1 = f32[1,18,16,128]{3,2,1,0:T(8,128)} custom-call(f32[1,16,8,128]{3,2,1,0:T(8,128)} %bitcast.18), custom_call_target="tpu_custom_call" | custom-call | tf_op jit(solution)/shard_map/halo3/pallas_call | solution.py:341
  78.4 23.7 %wall.1.wp_ref = f32[16,8,128]{2,1,0:T(8,128)} custom-call(s32[2]{0:T(128)} %pad_add_fusion.base_ref, s32[16,8,6]{2,1,0:T(8,128)} %copy.20.near_ref, f32[3,16,8,128]{3,2,1,0:T(8,128)} %own_ref.5, f32[18,16,128]{2,1,0:T(8,128)} %bitcast.15, s32[16,8,128]{2,1,0:T(8,128)} %live_ref.1, bf16[23040,128]{1,0:T(8,128)(2,1)} %get-tuple-element.25.rest_3_.fj_ref), custom_call_target="tpu_custom_call" | custom-call | tf_op jit(solution)/shard_map/wall/pallas_call | solution.py:549
  102.1 20.8 %scatter.1.partial_ref = f32[768,256]{1,0:T(8,128)} custom-call(f32[16,8,128]{2,1,0:T(8,128)} %wall.1.wp_ref, f32[3,16,8,128]{3,2,1,0:T(8,128)} %normal_ref.1, f32[3,16,8,128]{3,2,1,0:T(8,128)} %arm_ref.3, s32[16,8,128]{2,1,0:T(8,128)} %body_ref.3), custom_call_target="tpu_custom_call" | custom-call | tf_op jit(solution)/shard_map/scatter/pallas_call | solution.py:549
  122.9 0.0 copy-done.6
  122.9 0.0 copy-done.3
  123.0 0.0 copy-done.4
  123.0 0.0 copy-done.5
  123.0 0.0 copy-done.7
  123.0 0.2 pad_maximum_fusion
  123.2 0.2 reshape.40.params_ref
  123.4 0.0 copy-done.2
  123.4 0.0 copy-start
  123.4 1.1 copy-done
  124.5 27.6 %exchange.1 = (f32[6,128,256]{2,1,0:T(8,128)S(1)}, f32[6,32,256]{2,1,0:T(8,128)S(1)}, f32[1,128]{1,0:T(1,128)S(1)}) custom-call(f32[768,256]{1,0:T(8,128)S(1)} %copy-done, f32[8,128]{1,0:T(8,128)S(1)} %copy-done.2, f32[10,8,4,256]{3,2,1,0:T(4,128)S(1)} %reshape.40.params_ref), custom_call_target="tpu_custom_call" | custom-call | tf_op jit(solution)/shard_map/exchange/pallas_call | solution.py:512
  152.1 0.0 copy-start.1
  152.1 0.9 copy-done.1
  153.0 0.1 copy.22
  153.1 0.7 slice.22
  153.8 18.7 %gather.1 = f32[3,16,8,128]{3,2,1,0:T(8,128)} custom-call(f32[6,128,256]{2,1,0:T(8,128)} %copy-done.1, f32[3,16,8,128]{3,2,1,0:T(8,128)} %arm_ref.3, s32[16,8,128]{2,1,0:T(8,128)} %body_ref.3), custom_call_target="tpu_custom_call" | custom-call | tf_op jit(solution)/shard_map/gather/pallas_call | solution.py:549
  (1 shorter events, 0.0 us)
Async XLA Ops:
  47.8 75.2 %copy-start.6 = (f32[7680]{0:T(1024)S(1)}, f32[7680]{0:T(1024)}, u32[]{:S(2)}) copy-start(f32[7680]{0:T(1024)} %param.28) | copy-start | bytes 92164
  47.8 75.2 %copy-start.3 = (f32[3,7680]{1,0:T(4,128)S(1)}, f32[3,7680]{1,0:T(4,128)}, u32[]{:S(2)}) copy-start(f32[3,7680]{1,0:T(4,128)} %param.29) | copy-start | bytes 276484
  47.8 75.2 %copy-start.4 = (f32[3,7680]{1,0:T(4,128)S(1)}, f32[3,7680]{1,0:T(4,128)}, u32[]{:S(2)}) copy-start(f32[3,7680]{1,0:T(4,128)} %param.27) | copy-start | bytes 276484
  47.8 75.2 %copy-start.5 = (f32[3,7680]{1,0:T(4,128)S(1)}, f32[3,7680]{1,0:T(4,128)}, u32[]{:S(2)}) copy-start(f32[3,7680]{1,0:T(4,128)} %param.26) | copy-start | bytes 276484
  47.8 75.2 %copy-start.7 = (f32[10,512]{1,0:T(8,128)S(1)}, f32[10,512]{1,0:T(8,128)}, u32[]{:S(2)}) copy-start(f32[10,512]{1,0:T(8,128)} %constant.46.clone.1) | copy-start | bytes 61444
  71.8 51.6 %copy-start.2 = (f32[8,128]{1,0:T(8,128)S(1)}, f32[8,128]{1,0:T(8,128)}, u32[]{:S(2)}) copy-start(f32[8,128]{1,0:T(8,128)} %get-tuple-element.27.error_ref) | copy-start | bytes 12292
  123.4 1.1 copy-start
  152.1 0.9 copy-start.1
